TPU v7x, 32 devices: a whole 2x2x4 slice. The times are simulated.
32 devices in a mesh: section: 4 (over y, x), rep: 8 (over z, core).
Axes of the slice: x: 2, y: 2, z: 4, core: 2. Of those that a mesh axis runs over, the one named last changes fastest.
Arguments:
- x_in: bfloat16 [1024, 4096], P('rep'), may hold values from -6 to 6
- cot: bfloat16 [1024, 4096], P('rep'), may hold values from -6 to 6
- w_q: bfloat16 [4, 4096, 128], P('section', 'rep'), may hold values from -0.09375 to 0.09375
- w_k: bfloat16 [4, 4096, 128], P('section', 'rep'), may hold values from -0.09375 to 0.09375
- w_v: bfloat16 [4, 4096, 128], P('section', 'rep'), may hold values from -0.09375 to 0.09375
- w_out: bfloat16 [4, 4096, 128], P('section', 'rep'), may hold values from -0.5 to 0.5
- gains: float32 [4, 4096], P('section'), may hold values from 0.5 to 1.5
- offsets: int32 [4, 8], replicated, may hold values from 0 to 7
- counts: int32 [4, 8], replicated, may hold values from 1 to 8
Outputs:
- grad_q: float32 [4, 4096, 128], P('section', 'rep')
- grad_k: float32 [4, 4096, 128], P('section', 'rep')
- grad_v: float32 [4, 4096, 128], P('section', 'rep')
- grad_o: float32 [4, 4096, 128], P('section', 'rep')
All inputs are finite; a program needn't handle non-finite values.
Results may differ from a plain program's by a relative error of at most 0.023.
Values may be sent and summed in bfloat16 or wider, within the bound.
A program may use at most 64 MiB of HBM per device.

v0:
```python
import jax
import jax.numpy as jnp
from jax import lax
from jax.sharding import PartitionSpec as P

MB = 8
ROWS = 16


EPSILON = 1e-05


def from_behind(block, axis, distance):
    devices = range(lax.axis_size(axis))
    route = [(i - distance, i) for i in devices if i - distance in devices]
    return lax.ppermute(block, axis, route)


def attend(query, key, scale):
    rows_here = query.shape[0]
    scores = jnp.einsum("id,jd->ij", query, key, preferred_element_type=jnp.float32) * scale
    causal = jnp.arange(rows_here)[:, None] >= jnp.arange(rows_here)[None, :]
    expo = jnp.exp(jnp.where(causal, scores, -1e30))
    return expo / jnp.sum(expo, axis=-1, keepdims=True)


def forward_layer(layer_in, gain, weights, keep):
    weight_q, weight_k, weight_v, weight_o = weights
    scale = weight_q.shape[1] ** (-0.5)
    x_float = layer_in.astype(jnp.float32)
    rinv = lax.rsqrt(jnp.mean(x_float * x_float, axis=-1, keepdims=True) + EPSILON)
    normed = (x_float * rinv * gain).astype(jnp.bfloat16)
    query = jnp.dot(normed, weight_q, preferred_element_type=jnp.float32).astype(jnp.bfloat16)
    key = jnp.dot(normed, weight_k, preferred_element_type=jnp.float32).astype(jnp.bfloat16)
    value = jnp.dot(normed, weight_v, preferred_element_type=jnp.float32).astype(jnp.bfloat16)
    probs_low = attend(query, key, scale).astype(jnp.bfloat16)
    heads = jnp.dot(probs_low, value, preferred_element_type=jnp.float32).astype(jnp.bfloat16)
    output = lax.dot_general(
        heads, weight_o, (((1,), (1,)), ((), ())), preferred_element_type=jnp.float32
    )
    result = (x_float + keep * output).astype(jnp.bfloat16)
    return (result, normed, query, key, value, heads)


def backward_layer(grad_in, layer_in, query, key, value, gain, weights, keep):
    weight_q, weight_k, weight_v, weight_o = weights
    scale = weight_q.shape[1] ** (-0.5)
    grad_float = grad_in.astype(jnp.float32)
    grad_rows = (keep * grad_float).astype(jnp.bfloat16)
    d_heads = jnp.dot(grad_rows, weight_o, preferred_element_type=jnp.float32).astype(jnp.bfloat16)
    probs = attend(query, key, scale)
    probs_low = probs.astype(jnp.bfloat16)
    d_value = jnp.einsum(
        "ij,id->jd", probs_low, d_heads, preferred_element_type=jnp.float32
    ).astype(jnp.bfloat16)
    d_probs = jnp.einsum("id,jd->ij", d_heads, value, preferred_element_type=jnp.float32)
    d_score = (probs * (d_probs - jnp.sum(probs * d_probs, axis=-1, keepdims=True)) * scale).astype(
        jnp.bfloat16
    )
    d_query = jnp.dot(d_score, key, preferred_element_type=jnp.float32).astype(jnp.bfloat16)
    d_key = jnp.einsum("ij,id->jd", d_score, query, preferred_element_type=jnp.float32).astype(
        jnp.bfloat16
    )
    contract = (((1,), (1,)), ((), ()))
    d_normed = lax.dot_general(d_query, weight_q, contract, preferred_element_type=jnp.float32)
    d_normed = d_normed + lax.dot_general(
        d_key, weight_k, contract, preferred_element_type=jnp.float32
    )
    d_normed = d_normed + lax.dot_general(
        d_value, weight_v, contract, preferred_element_type=jnp.float32
    )
    x_float = layer_in.astype(jnp.float32)
    rinv = lax.rsqrt(jnp.mean(x_float * x_float, axis=-1, keepdims=True) + EPSILON)
    scaled = d_normed * gain
    d_input = rinv * (
        scaled - x_float * rinv * rinv * jnp.mean(scaled * x_float, axis=-1, keepdims=True)
    )
    return ((grad_float + d_input).astype(jnp.bfloat16), grad_rows, d_query, d_key, d_value)


def store_slot(store, value, slot_at, is_valid):
    old_value = lax.dynamic_index_in_dim(store, slot_at, 0, keepdims=False)
    fresh = jnp.where(is_valid, value, old_value)
    return lax.dynamic_update_index_in_dim(store, fresh, slot_at, 0)


def zeros_like_all(values):
    return tuple((jnp.zeros(value.shape, value.dtype) for value in values))


def pick_slot(store, slot_at):
    return lax.dynamic_index_in_dim(store, slot_at, 0, keepdims=False)


def local_grad(left, right):
    width_left = left.shape[-1]
    width_right = right.shape[-1]
    return jnp.einsum(
        "td,th->dh",
        left.reshape(-1, width_left),
        right.reshape(-1, width_right),
        preferred_element_type=jnp.float32,
    )


def on_device(x_in, cot, w_q, w_k, w_v, w_out, gains, offsets, counts):
    section_count = lax.axis_size("section")
    rep_count = lax.axis_size("rep")
    section_pos = lax.axis_index("section")
    rep_pos = lax.axis_index("rep")
    weights = (
        lax.all_gather(w_q[0], "rep", axis=0, tiled=True),
        lax.all_gather(w_k[0], "rep", axis=0, tiled=True),
        lax.all_gather(w_v[0], "rep", axis=0, tiled=True),
        lax.all_gather(w_out[0], "rep", axis=0, tiled=True),
    )
    width = weights[0].shape[0]
    head_size = weights[0].shape[1]
    gain = gains[0]
    landing_sum = jnp.cumsum(offsets, axis=0) % rep_count
    my_offsets = lax.dynamic_index_in_dim(landing_sum, section_pos, 0, keepdims=False)
    landing = (rep_pos + my_offsets) % rep_count
    count_row = lax.dynamic_index_in_dim(counts, section_pos, 0, keepdims=False)
    match_rep = landing[:, None] == jnp.arange(rep_count, dtype=jnp.int32)[None, :]
    allowed = jnp.sum(jnp.where(match_rep, count_row[None, :], 0), axis=1)
    keeps = (jnp.arange(MB, dtype=jnp.int32) < allowed).astype(jnp.float32)
    inputs = x_in.reshape(MB, ROWS, width)
    top_grads = cot.reshape(MB, ROWS, width)
    tick_count = section_count + MB - 1
    row_block = jnp.zeros((ROWS, width), jnp.bfloat16)
    head_block = jnp.zeros((ROWS, head_size), jnp.bfloat16)

    def forward_tick(tick_no, carry):
        inbox, saved_in, saved_normed, saved_q, saved_k, saved_v, saved_heads = carry
        batch_pos = tick_no - section_pos
        is_valid = (batch_pos >= 0) & (batch_pos < MB)
        batch_at = jnp.clip(batch_pos, 0, MB - 1)
        own_rows = pick_slot(inputs, batch_at)
        layer_in = jnp.where(section_pos == 0, own_rows, inbox)
        keep = pick_slot(keeps, batch_at)
        blank = (row_block, row_block, head_block, head_block, head_block, head_block)
        made = lax.cond(
            is_valid,
            lambda rows_in: forward_layer(rows_in, gain, weights, keep),
            lambda rows_in: zeros_like_all(blank),
            layer_in,
        )
        result, normed, query, key, value, heads = made
        saved_in = store_slot(saved_in, layer_in, batch_at, is_valid)
        saved_normed = store_slot(saved_normed, normed, batch_at, is_valid)
        saved_q = store_slot(saved_q, query, batch_at, is_valid)
        saved_k = store_slot(saved_k, key, batch_at, is_valid)
        saved_v = store_slot(saved_v, value, batch_at, is_valid)
        saved_heads = store_slot(saved_heads, heads, batch_at, is_valid)
        inbox = from_behind(result, "section", 1)
        return (inbox, saved_in, saved_normed, saved_q, saved_k, saved_v, saved_heads)

    wide_store = jnp.zeros((MB, ROWS, width), jnp.bfloat16)
    head_store = jnp.zeros((MB, ROWS, head_size), jnp.bfloat16)
    start_fwd = (row_block, wide_store, wide_store, head_store, head_store, head_store, head_store)
    _, saved_in, saved_normed, saved_q, saved_k, saved_v, saved_heads = lax.fori_loop(
        0, tick_count, forward_tick, start_fwd
    )

    def backward_tick(tick_no, carry):
        inbox, saved_rows, saved_dq, saved_dk, saved_dv = carry
        batch_pos = tick_no - (section_count - 1 - section_pos)
        is_valid = (batch_pos >= 0) & (batch_pos < MB)
        batch_at = jnp.clip(batch_pos, 0, MB - 1)
        grad_in = jnp.where(section_pos == section_count - 1, pick_slot(top_grads, batch_at), inbox)
        layer_in = pick_slot(saved_in, batch_at)
        query = pick_slot(saved_q, batch_at)
        key = pick_slot(saved_k, batch_at)
        value = pick_slot(saved_v, batch_at)
        keep = pick_slot(keeps, batch_at)
        blank = (row_block, row_block, head_block, head_block, head_block)
        made = lax.cond(
            is_valid,
            lambda rows_in: backward_layer(
                rows_in, layer_in, query, key, value, gain, weights, keep
            ),
            lambda rows_in: zeros_like_all(blank),
            grad_in,
        )
        grad_back, grad_rows, d_query, d_key, d_value = made
        saved_rows = store_slot(saved_rows, grad_rows, batch_at, is_valid)
        saved_dq = store_slot(saved_dq, d_query, batch_at, is_valid)
        saved_dk = store_slot(saved_dk, d_key, batch_at, is_valid)
        saved_dv = store_slot(saved_dv, d_value, batch_at, is_valid)
        inbox = from_behind(grad_back, "section", -1)
        return (inbox, saved_rows, saved_dq, saved_dk, saved_dv)

    start_bwd = (row_block, wide_store, head_store, head_store, head_store)
    _, saved_rows, saved_dq, saved_dk, saved_dv = lax.fori_loop(
        0, tick_count, backward_tick, start_bwd
    )
    full_q = local_grad(saved_normed, saved_dq)
    full_k = local_grad(saved_normed, saved_dk)
    full_v = local_grad(saved_normed, saved_dv)
    full_o = local_grad(saved_rows, saved_heads)
    share_width = width // rep_count
    totals = (
        lax.psum(full_q.astype(jnp.bfloat16), "rep").astype(jnp.float32),
        lax.psum(full_k.astype(jnp.bfloat16), "rep").astype(jnp.float32),
        lax.psum(full_v.astype(jnp.bfloat16), "rep").astype(jnp.float32),
        lax.psum(full_o.astype(jnp.bfloat16), "rep").astype(jnp.float32),
    )
    parts = tuple(
        (lax.dynamic_slice_in_dim(total, rep_pos * share_width, share_width, 0) for total in totals)
    )
    return (parts[0][None], parts[1][None], parts[2][None], parts[3][None])


def solution(mesh):
    in_specs = (
        P("rep", None),
        P("rep", None),
        P("section", "rep", None),
        P("section", "rep", None),
        P("section", "rep", None),
        P("section", "rep", None),
        P("section", None),
        P(),
        P(),
    )
    out_specs = (
        P("section", "rep", None),
        P("section", "rep", None),
        P("section", "rep", None),
        P("section", "rep", None),
    )
    return jax.shard_map(
        on_device, mesh=mesh, in_specs=in_specs, out_specs=out_specs, check_vma=False
    )
```

profile of v0, /device:TPU:0, one launch (start us, length us, event | category | flops | bytes accessed | tf_op | source)
XLA Modules:
  0.0 682.0 jit_solution(16594448629739413946)
XLA Ops:
  11.5 23.1 %all-gather.9.cloned.1.call-done = bf16[1,4096,128]{2,1,0:T(8,128)(2,1)} async-done(((bf16[1,512,128]{2,1,0:T(8,128)(2,1)}), bf16[1,4096,128]{2,1,0:T(8,128)(2,1)}) %all-gather.9.cloned.1.call-update) | async-done | bytes 1048592 | tf_op jit(solution)/shard_map/all_gather | solution.py:112
  34.6 23.5 %all-gather.11.cloned.1.call-done = bf16[1,4096,128]{2,1,0:T(8,128)(2,1)} async-done(((bf16[1,512,128]{2,1,0:T(8,128)(2,1)}), bf16[1,4096,128]{2,1,0:T(8,128)(2,1)}) %all-gather.11.cloned.1.call-update) | async-done | bytes 1048592 | tf_op jit(solution)/shard_map/all_gather | solution.py:113
  58.1 23.5 %all-gather.13.cloned.1.call-done = bf16[1,4096,128]{2,1,0:T(8,128)(2,1)} async-done(((bf16[1,512,128]{2,1,0:T(8,128)(2,1)}), bf16[1,4096,128]{2,1,0:T(8,128)(2,1)}) %all-gather.13.cloned.1.call-update) | async-done | bytes 1048592 | tf_op jit(solution)/shard_map/all_gather | solution.py:114
  81.6 23.3 %all-gather.15.cloned.1.call-done = bf16[1,4096,128]{2,1,0:T(8,128)(2,1)} async-done(((bf16[1,512,128]{2,1,0:T(8,128)(2,1)}), bf16[1,4096,128]{2,1,0:T(8,128)(2,1)}) %all-gather.15.cloned.1.call-update) | async-done | bytes 1048592 | tf_op jit(solution)/shard_map/all_gather | solution.py:115
  109.6 211.7 %while.49 = (s32[]{:T(128)}, bf16[16,4096]{1,0:T(8,128)(2,1)S(1)}, bf16[8,16,4096]{2,1,0:T(8,128)(2,1)}, bf16[8,16,4096]{2,1,0:T(8,128)(2,1)}, bf16[8,16,128]{2,...) while((s32[]{:T(128)}, bf16[16,4096]{1,0:T(8,128)(2,1)S(1)}, ...), condition=%wide.region_7.8_spmd, body=%wide.region_2.7_spmd.sunk | while | flops 68175368 | bytes 16946660 | solution.py:161
  112.2 8.9 %conditional.4 = (bf16[16,4096]{1,0:T(8,128)(2,1)}, bf16[16,4096]{1,0:T(8,128)(2,1)S(1)}, bf16[16,128]{1,0:T(8,128)(2,1)}, bf16[16,128]{1,0:T(8,128)(2,1)S(1)}, ...) conditional(s32[]{:T(128)} %convert_element_type.174, () %tuple.109, (bf16[16,4096]{1,0:T(8,128)(2,1)S(1)}, ...), branch_computations={%region_3.3_spmd, %region_4.6_spmd} | conditional | flops 67970560 | bytes 14764648 | solution.py:142
  118.7 2.3 fusion.1
  131.8 8.9 %conditional.4 = (bf16[16,4096]{1,0:T(8,128)(2,1)}, bf16[16,4096]{1,0:T(8,128)(2,1)S(1)}, bf16[16,128]{1,0:T(8,128)(2,1)}, bf16[16,128]{1,0:T(8,128)(2,1)S(1)}, ...) conditional(s32[]{:T(128)} %convert_element_type.174, () %tuple.109, (bf16[16,4096]{1,0:T(8,128)(2,1)S(1)}, ...), branch_computations={%region_3.3_spmd, %region_4.6_spmd} | conditional | flops 67970560 | bytes 14764648 | solution.py:142
  138.3 2.3 fusion.1
  151.5 8.9 %conditional.4 = (bf16[16,4096]{1,0:T(8,128)(2,1)}, bf16[16,4096]{1,0:T(8,128)(2,1)S(1)}, bf16[16,128]{1,0:T(8,128)(2,1)}, bf16[16,128]{1,0:T(8,128)(2,1)S(1)}, ...) conditional(s32[]{:T(128)} %convert_element_type.174, () %tuple.109, (bf16[16,4096]{1,0:T(8,128)(2,1)S(1)}, ...), branch_computations={%region_3.3_spmd, %region_4.6_spmd} | conditional | flops 67970560 | bytes 14764648 | solution.py:142
  158.0 2.3 fusion.1
  171.5 8.9 %conditional.4 = (bf16[16,4096]{1,0:T(8,128)(2,1)}, bf16[16,4096]{1,0:T(8,128)(2,1)S(1)}, bf16[16,128]{1,0:T(8,128)(2,1)}, bf16[16,128]{1,0:T(8,128)(2,1)S(1)}, ...) conditional(s32[]{:T(128)} %convert_element_type.174, () %tuple.109, (bf16[16,4096]{1,0:T(8,128)(2,1)S(1)}, ...), branch_computations={%region_3.3_spmd, %region_4.6_spmd} | conditional | flops 67970560 | bytes 14764648 | solution.py:142
  178.0 2.3 fusion.1
  180.3 1.9 collective-permute-start
  191.8 8.9 %conditional.4 = (bf16[16,4096]{1,0:T(8,128)(2,1)}, bf16[16,4096]{1,0:T(8,128)(2,1)S(1)}, bf16[16,128]{1,0:T(8,128)(2,1)}, bf16[16,128]{1,0:T(8,128)(2,1)S(1)}, ...) conditional(s32[]{:T(128)} %convert_element_type.174, () %tuple.109, (bf16[16,4096]{1,0:T(8,128)(2,1)S(1)}, ...), branch_computations={%region_3.3_spmd, %region_4.6_spmd} | conditional | flops 67970560 | bytes 14764648 | solution.py:142
  198.3 2.3 fusion.1
  212.0 8.9 %conditional.4 = (bf16[16,4096]{1,0:T(8,128)(2,1)}, bf16[16,4096]{1,0:T(8,128)(2,1)S(1)}, bf16[16,128]{1,0:T(8,128)(2,1)}, bf16[16,128]{1,0:T(8,128)(2,1)S(1)}, ...) conditional(s32[]{:T(128)} %convert_element_type.174, () %tuple.109, (bf16[16,4096]{1,0:T(8,128)(2,1)S(1)}, ...), branch_computations={%region_3.3_spmd, %region_4.6_spmd} | conditional | flops 67970560 | bytes 14764648 | solution.py:142
  218.5 2.3 fusion.1
  220.9 1.9 collective-permute-start
  232.2 8.9 %conditional.4 = (bf16[16,4096]{1,0:T(8,128)(2,1)}, bf16[16,4096]{1,0:T(8,128)(2,1)S(1)}, bf16[16,128]{1,0:T(8,128)(2,1)}, bf16[16,128]{1,0:T(8,128)(2,1)S(1)}, ...) conditional(s32[]{:T(128)} %convert_element_type.174, () %tuple.109, (bf16[16,4096]{1,0:T(8,128)(2,1)S(1)}, ...), branch_computations={%region_3.3_spmd, %region_4.6_spmd} | conditional | flops 67970560 | bytes 14764648 | solution.py:142
  238.8 2.3 fusion.1
  241.1 1.9 collective-permute-start
  252.5 8.9 %conditional.4 = (bf16[16,4096]{1,0:T(8,128)(2,1)}, bf16[16,4096]{1,0:T(8,128)(2,1)S(1)}, bf16[16,128]{1,0:T(8,128)(2,1)}, bf16[16,128]{1,0:T(8,128)(2,1)S(1)}, ...) conditional(s32[]{:T(128)} %convert_element_type.174, () %tuple.109, (bf16[16,4096]{1,0:T(8,128)(2,1)S(1)}, ...), branch_computations={%region_3.3_spmd, %region_4.6_spmd} | conditional | flops 67970560 | bytes 14764648 | solution.py:142
  259.1 2.3 fusion.1
  272.8 2.4 conditional.4
  275.2 8.3 %collective-permute-start = (bf16[16,4096]{1,0:T(8,128)(2,1)}, bf16[16,4096]{1,0:T(8,128)(2,1)S(1)}, u32[]{:S(2)}, u32[]{:S(2)}) collective-permute-start(bf16[16,4096]{1,0:T(8,128)(2,1)} %get-tuple-element.1244), channel_id=1, source_target_pairs={{0,8},{8,16},{16,24},{1,9},{9,17},{17,25},{2,10},{10,18},{18,26},{... | collective-permute-start | bytes 393224 | tf_op jit(solution)/shard_map/while/body/eval_jaxpr/ppermute | solution.py:16
  291.7 2.4 conditional.4
  294.1 3.3 collective-permute-start
  305.5 2.4 conditional.4
  308.0 7.8 %collective-permute-start = (bf16[16,4096]{1,0:T(8,128)(2,1)}, bf16[16,4096]{1,0:T(8,128)(2,1)S(1)}, u32[]{:S(2)}, u32[]{:S(2)}) collective-permute-start(bf16[16,4096]{1,0:T(8,128)(2,1)} %get-tuple-element.1244), channel_id=1, source_target_pairs={{0,8},{8,16},{16,24},{1,9},{9,17},{17,25},{2,10},{10,18},{18,26},{... | collective-permute-start | bytes 393224 | tf_op jit(solution)/shard_map/while/body/eval_jaxpr/ppermute | solution.py:16
  324.3 241.3 %while.50 = (s32[]{:T(128)}, bf16[16,4096]{1,0:T(8,128)(2,1)S(1)}, bf16[8,16,4096]{2,1,0:T(8,128)(2,1)}, bf16[8,16,128]{2,1,0:T(8,128)(2,1)}, bf16[8,16,128]{2,1...) while((s32[]{:T(128)}, bf16[16,4096]{1,0:T(8,128)(2,1)S(1)}, ...), condition=%wide.region_15.16_spmd, body=%wide.region_8.15_spmd.sunk | while | flops 68961784 | bytes 9356268 | solution.py:194
  324.3 1.9 conditional.5
  333.6 1.9 conditional.5
  344.2 1.9 conditional.5
  353.5 33.2 %collective-permute-done.1 = bf16[16,4096]{1,0:T(8,128)(2,1)S(1)} collective-permute-done((bf16[16,4096]{1,0:T(8,128)(2,1)}, bf16[16,4096]{1,0:T(8,128)(2,1)S(1)}, u32[]{:S(2)}, u32[]{:S(2)}) %collective-permute-start.1) | collective-permute-done | bytes 131104 | tf_op jit(solution)/shard_map/while/body/eval_jaxpr/ppermute | solution.py:16
  386.7 13.7 %conditional.5 = (bf16[16,4096]{1,0:T(8,128)(2,1)}, bf16[16,4096]{1,0:T(8,128)(2,1)S(1)}, bf16[16,128]{1,0:T(8,128)(2,1)S(1)}, bf16[16,128]{1,0:T(8,128)(2,1)}, bf16[16,128]{1,0:T(8,128)(2,1)}) conditional(s32[]{:T(128)} %convert_element_type.175, () %tuple.113, (pred[]{:T(512)}, bf16[8,16,4096]{2,1,0:T(8,128)(2,1)}, s32[]{:T(128)}, ...), branch_computations={%region_9.9_spmd, %region_10.14_spmd} | conditional | flops 68890096 | bytes 8113206 | solution.py:177
  409.1 13.7 %conditional.5 = (bf16[16,4096]{1,0:T(8,128)(2,1)}, bf16[16,4096]{1,0:T(8,128)(2,1)S(1)}, bf16[16,128]{1,0:T(8,128)(2,1)S(1)}, bf16[16,128]{1,0:T(8,128)(2,1)}, bf16[16,128]{1,0:T(8,128)(2,1)}) conditional(s32[]{:T(128)} %convert_element_type.175, () %tuple.113, (pred[]{:T(512)}, bf16[8,16,4096]{2,1,0:T(8,128)(2,1)}, s32[]{:T(128)}, ...), branch_computations={%region_9.9_spmd, %region_10.14_spmd} | conditional | flops 68890096 | bytes 8113206 | solution.py:177
  431.6 13.7 %conditional.5 = (bf16[16,4096]{1,0:T(8,128)(2,1)}, bf16[16,4096]{1,0:T(8,128)(2,1)S(1)}, bf16[16,128]{1,0:T(8,128)(2,1)S(1)}, bf16[16,128]{1,0:T(8,128)(2,1)}, bf16[16,128]{1,0:T(8,128)(2,1)}) conditional(s32[]{:T(128)} %convert_element_type.175, () %tuple.113, (pred[]{:T(512)}, bf16[8,16,4096]{2,1,0:T(8,128)(2,1)}, s32[]{:T(128)}, ...), branch_computations={%region_9.9_spmd, %region_10.14_spmd} | conditional | flops 68890096 | bytes 8113206 | solution.py:177
  454.0 13.7 %conditional.5 = (bf16[16,4096]{1,0:T(8,128)(2,1)}, bf16[16,4096]{1,0:T(8,128)(2,1)S(1)}, bf16[16,128]{1,0:T(8,128)(2,1)S(1)}, bf16[16,128]{1,0:T(8,128)(2,1)}, bf16[16,128]{1,0:T(8,128)(2,1)}) conditional(s32[]{:T(128)} %convert_element_type.175, () %tuple.113, (pred[]{:T(512)}, bf16[8,16,4096]{2,1,0:T(8,128)(2,1)}, s32[]{:T(128)}, ...), branch_computations={%region_9.9_spmd, %region_10.14_spmd} | conditional | flops 68890096 | bytes 8113206 | solution.py:177
  476.4 13.7 %conditional.5 = (bf16[16,4096]{1,0:T(8,128)(2,1)}, bf16[16,4096]{1,0:T(8,128)(2,1)S(1)}, bf16[16,128]{1,0:T(8,128)(2,1)S(1)}, bf16[16,128]{1,0:T(8,128)(2,1)}, bf16[16,128]{1,0:T(8,128)(2,1)}) conditional(s32[]{:T(128)} %convert_element_type.175, () %tuple.113, (pred[]{:T(512)}, bf16[8,16,4096]{2,1,0:T(8,128)(2,1)}, s32[]{:T(128)}, ...), branch_computations={%region_9.9_spmd, %region_10.14_spmd} | conditional | flops 68890096 | bytes 8113206 | solution.py:177
  498.9 13.7 %conditional.5 = (bf16[16,4096]{1,0:T(8,128)(2,1)}, bf16[16,4096]{1,0:T(8,128)(2,1)S(1)}, bf16[16,128]{1,0:T(8,128)(2,1)S(1)}, bf16[16,128]{1,0:T(8,128)(2,1)}, bf16[16,128]{1,0:T(8,128)(2,1)}) conditional(s32[]{:T(128)} %convert_element_type.175, () %tuple.113, (pred[]{:T(512)}, bf16[8,16,4096]{2,1,0:T(8,128)(2,1)}, s32[]{:T(128)}, ...), branch_computations={%region_9.9_spmd, %region_10.14_spmd} | conditional | flops 68890096 | bytes 8113206 | solution.py:177
  521.3 13.7 %conditional.5 = (bf16[16,4096]{1,0:T(8,128)(2,1)}, bf16[16,4096]{1,0:T(8,128)(2,1)S(1)}, bf16[16,128]{1,0:T(8,128)(2,1)S(1)}, bf16[16,128]{1,0:T(8,128)(2,1)}, bf16[16,128]{1,0:T(8,128)(2,1)}) conditional(s32[]{:T(128)} %convert_element_type.175, () %tuple.113, (pred[]{:T(512)}, bf16[8,16,4096]{2,1,0:T(8,128)(2,1)}, s32[]{:T(128)}, ...), branch_computations={%region_9.9_spmd, %region_10.14_spmd} | conditional | flops 68890096 | bytes 8113206 | solution.py:177
  543.7 13.7 %conditional.5 = (bf16[16,4096]{1,0:T(8,128)(2,1)}, bf16[16,4096]{1,0:T(8,128)(2,1)S(1)}, bf16[16,128]{1,0:T(8,128)(2,1)S(1)}, bf16[16,128]{1,0:T(8,128)(2,1)}, bf16[16,128]{1,0:T(8,128)(2,1)}) conditional(s32[]{:T(128)} %convert_element_type.175, () %tuple.113, (pred[]{:T(512)}, bf16[8,16,4096]{2,1,0:T(8,128)(2,1)}, s32[]{:T(128)}, ...), branch_computations={%region_9.9_spmd, %region_10.14_spmd} | conditional | flops 68890096 | bytes 8113206 | solution.py:177
  565.6 2.7 fusion.37
  568.3 2.7 fusion.36
  571.0 2.7 fusion.35
  573.7 2.2 fusion.38
  576.0 96.0 %all-reduce.3.cloned.1.call-done = (bf16[4096,128]{1,0:T(8,128)(2,1)}, bf16[4096,128]{1,0:T(8,128)(2,1)}, bf16[4096,128]{1,0:T(8,128)(2,1)}, bf16[4096,128]{1,0:T(8,128)(2,1)}) async-done(((bf16[4096,128]{1,0:T(8,128)(2,1)}, bf16[4096,128]{1,0:T(8,128)(2,1)}, bf16[4096,128]{1,0:T(8,128)(2,1)}, bf16[4096,128]{1,0:T(8,128)(2,1)}), (bf16[4096,128]{1,0:T(8,128)(2,1)}, bf16[4096,128]{1,0:T(8,128)(2,1)}, ...) | async-done | bytes 4194320 | tf_op jit(solution)/shard_map/psum | solution.py:203
  (645 shorter events, 390.3 us)
Async XLA Ops:
  7.2 27.5 %all-gather.9.cloned.1.call-start = ((), (), s32[]{:S(2)}) async-start(), calls=%async_computation | async-start | bytes 1179648 | tf_op jit(solution)/shard_map/all_gather | solution.py:112
  7.9 50.2 %all-gather.11.cloned.1.call-start = ((), (), s32[]{:S(2)}) async-start(), calls=%async_computation.1 | async-start | bytes 1179648 | tf_op jit(solution)/shard_map/all_gather | solution.py:113
  8.7 72.9 %all-gather.13.cloned.1.call-start = ((), (), s32[]{:S(2)}) async-start(), calls=%async_computation.2 | async-start | bytes 1179648 | tf_op jit(solution)/shard_map/all_gather | solution.py:114
  9.4 95.5 %all-gather.15.cloned.1.call-start = ((), (), s32[]{:S(2)}) async-start(), calls=%async_computation.3 | async-start | bytes 1179648 | tf_op jit(solution)/shard_map/all_gather | solution.py:115
  10.0 661.9 %all-reduce.3.cloned.1.call-start = ((), (), s32[]{:S(2)}) async-start(), calls=%async_computation.4 | async-start | bytes 8388608 | tf_op jit(solution)/shard_map/psum | solution.py:203
  104.9 4.7 copy-start.1
  104.9 4.7 copy-start.2
  113.4 5.3 copy-start.5
  116.0 5.1 copy-start.7
  121.0 8.2 %collective-permute-start = (bf16[16,4096]{1,0:T(8,128)(2,1)}, bf16[16,4096]{1,0:T(8,128)(2,1)S(1)}, u32[]{:S(2)}, u32[]{:S(2)}) collective-permute-start(bf16[16,4096]{1,0:T(8,128)(2,1)} %get-tuple-element.1244), channel_id=1, source_target_pairs={{0,8},{8,16},{16,24},{1,9},{9,17},{17,25},{2,10},{10,18},{18,26},{... | collective-permute-start | bytes 393224 | tf_op jit(solution)/shard_map/while/body/eval_jaxpr/ppermute | solution.py:16
  133.1 5.3 copy-start.5
  135.6 5.1 copy-start.7
  140.7 8.2 %collective-permute-start = (bf16[16,4096]{1,0:T(8,128)(2,1)}, bf16[16,4096]{1,0:T(8,128)(2,1)S(1)}, u32[]{:S(2)}, u32[]{:S(2)}) collective-permute-start(bf16[16,4096]{1,0:T(8,128)(2,1)} %get-tuple-element.1244), channel_id=1, source_target_pairs={{0,8},{8,16},{16,24},{1,9},{9,17},{17,25},{2,10},{10,18},{18,26},{... | collective-permute-start | bytes 393224 | tf_op jit(solution)/shard_map/while/body/eval_jaxpr/ppermute | solution.py:16
  152.7 5.3 copy-start.5
  155.2 5.1 copy-start.7
  160.3 8.6 %collective-permute-start = (bf16[16,4096]{1,0:T(8,128)(2,1)}, bf16[16,4096]{1,0:T(8,128)(2,1)S(1)}, u32[]{:S(2)}, u32[]{:S(2)}) collective-permute-start(bf16[16,4096]{1,0:T(8,128)(2,1)} %get-tuple-element.1244), channel_id=1, source_target_pairs={{0,8},{8,16},{16,24},{1,9},{9,17},{17,25},{2,10},{10,18},{18,26},{... | collective-permute-start | bytes 393224 | tf_op jit(solution)/shard_map/while/body/eval_jaxpr/ppermute | solution.py:16
  172.7 5.3 copy-start.5
  175.3 5.1 copy-start.7
  180.3 8.9 %collective-permute-start = (bf16[16,4096]{1,0:T(8,128)(2,1)}, bf16[16,4096]{1,0:T(8,128)(2,1)S(1)}, u32[]{:S(2)}, u32[]{:S(2)}) collective-permute-start(bf16[16,4096]{1,0:T(8,128)(2,1)} %get-tuple-element.1244), channel_id=1, source_target_pairs={{0,8},{8,16},{16,24},{1,9},{9,17},{17,25},{2,10},{10,18},{18,26},{... | collective-permute-start | bytes 393224 | tf_op jit(solution)/shard_map/while/body/eval_jaxpr/ppermute | solution.py:16
  193.0 5.3 copy-start.5
  195.6 5.1 copy-start.7
  200.6 8.8 %collective-permute-start = (bf16[16,4096]{1,0:T(8,128)(2,1)}, bf16[16,4096]{1,0:T(8,128)(2,1)S(1)}, u32[]{:S(2)}, u32[]{:S(2)}) collective-permute-start(bf16[16,4096]{1,0:T(8,128)(2,1)} %get-tuple-element.1244), channel_id=1, source_target_pairs={{0,8},{8,16},{16,24},{1,9},{9,17},{17,25},{2,10},{10,18},{18,26},{... | collective-permute-start | bytes 393224 | tf_op jit(solution)/shard_map/while/body/eval_jaxpr/ppermute | solution.py:16
  213.2 5.3 copy-start.5
  215.8 5.1 copy-start.7
  220.9 8.8 %collective-permute-start = (bf16[16,4096]{1,0:T(8,128)(2,1)}, bf16[16,4096]{1,0:T(8,128)(2,1)S(1)}, u32[]{:S(2)}, u32[]{:S(2)}) collective-permute-start(bf16[16,4096]{1,0:T(8,128)(2,1)} %get-tuple-element.1244), channel_id=1, source_target_pairs={{0,8},{8,16},{16,24},{1,9},{9,17},{17,25},{2,10},{10,18},{18,26},{... | collective-permute-start | bytes 393224 | tf_op jit(solution)/shard_map/while/body/eval_jaxpr/ppermute | solution.py:16
  233.5 5.3 copy-start.5
  236.0 5.1 copy-start.7
  241.1 8.9 %collective-permute-start = (bf16[16,4096]{1,0:T(8,128)(2,1)}, bf16[16,4096]{1,0:T(8,128)(2,1)S(1)}, u32[]{:S(2)}, u32[]{:S(2)}) collective-permute-start(bf16[16,4096]{1,0:T(8,128)(2,1)} %get-tuple-element.1244), channel_id=1, source_target_pairs={{0,8},{8,16},{16,24},{1,9},{9,17},{17,25},{2,10},{10,18},{18,26},{... | collective-permute-start | bytes 393224 | tf_op jit(solution)/shard_map/while/body/eval_jaxpr/ppermute | solution.py:16
  253.8 5.3 copy-start.5
  256.3 5.1 copy-start.7
  261.4 8.8 %collective-permute-start = (bf16[16,4096]{1,0:T(8,128)(2,1)}, bf16[16,4096]{1,0:T(8,128)(2,1)S(1)}, u32[]{:S(2)}, u32[]{:S(2)}) collective-permute-start(bf16[16,4096]{1,0:T(8,128)(2,1)} %get-tuple-element.1244), channel_id=1, source_target_pairs={{0,8},{8,16},{16,24},{1,9},{9,17},{17,25},{2,10},{10,18},{18,26},{... | collective-permute-start | bytes 393224 | tf_op jit(solution)/shard_map/while/body/eval_jaxpr/ppermute | solution.py:16
  275.2 13.9 %collective-permute-start = (bf16[16,4096]{1,0:T(8,128)(2,1)}, bf16[16,4096]{1,0:T(8,128)(2,1)S(1)}, u32[]{:S(2)}, u32[]{:S(2)}) collective-permute-start(bf16[16,4096]{1,0:T(8,128)(2,1)} %get-tuple-element.1244), channel_id=1, source_target_pairs={{0,8},{8,16},{16,24},{1,9},{9,17},{17,25},{2,10},{10,18},{18,26},{... | collective-permute-start | bytes 393224 | tf_op jit(solution)/shard_map/while/body/eval_jaxpr/ppermute | solution.py:16
  294.1 8.8 %collective-permute-start = (bf16[16,4096]{1,0:T(8,128)(2,1)}, bf16[16,4096]{1,0:T(8,128)(2,1)S(1)}, u32[]{:S(2)}, u32[]{:S(2)}) collective-permute-start(bf16[16,4096]{1,0:T(8,128)(2,1)} %get-tuple-element.1244), channel_id=1, source_target_pairs={{0,8},{8,16},{16,24},{1,9},{9,17},{17,25},{2,10},{10,18},{18,26},{... | collective-permute-start | bytes 393224 | tf_op jit(solution)/shard_map/while/body/eval_jaxpr/ppermute | solution.py:16
  308.0 13.4 %collective-permute-start = (bf16[16,4096]{1,0:T(8,128)(2,1)}, bf16[16,4096]{1,0:T(8,128)(2,1)S(1)}, u32[]{:S(2)}, u32[]{:S(2)}) collective-permute-start(bf16[16,4096]{1,0:T(8,128)(2,1)} %get-tuple-element.1244), channel_id=1, source_target_pairs={{0,8},{8,16},{16,24},{1,9},{9,17},{17,25},{2,10},{10,18},{18,26},{... | collective-permute-start | bytes 393224 | tf_op jit(solution)/shard_map/while/body/eval_jaxpr/ppermute | solution.py:16
  326.2 7.4 %collective-permute-start.1 = (bf16[16,4096]{1,0:T(8,128)(2,1)}, bf16[16,4096]{1,0:T(8,128)(2,1)S(1)}, u32[]{:S(2)}, u32[]{:S(2)}) collective-permute-start(bf16[16,4096]{1,0:T(8,128)(2,1)} %get-tuple-element.1274), channel_id=1, source_target_pairs={{8,0},{16,8},{24,16},{9,1},{17,9},{25,17},{10,2},{18,10},{26,18},{... | collective-permute-start | bytes 393224 | tf_op jit(solution)/shard_map/while/body/eval_jaxpr/ppermute | solution.py:16
  335.5 8.7 %collective-permute-start.1 = (bf16[16,4096]{1,0:T(8,128)(2,1)}, bf16[16,4096]{1,0:T(8,128)(2,1)S(1)}, u32[]{:S(2)}, u32[]{:S(2)}) collective-permute-start(bf16[16,4096]{1,0:T(8,128)(2,1)} %get-tuple-element.1274), channel_id=1, source_target_pairs={{8,0},{16,8},{24,16},{9,1},{17,9},{25,17},{10,2},{18,10},{26,18},{... | collective-permute-start | bytes 393224 | tf_op jit(solution)/shard_map/while/body/eval_jaxpr/ppermute | solution.py:16
  346.1 40.6 %collective-permute-start.1 = (bf16[16,4096]{1,0:T(8,128)(2,1)}, bf16[16,4096]{1,0:T(8,128)(2,1)S(1)}, u32[]{:S(2)}, u32[]{:S(2)}) collective-permute-start(bf16[16,4096]{1,0:T(8,128)(2,1)} %get-tuple-element.1274), channel_id=1, source_target_pairs={{8,0},{16,8},{24,16},{9,1},{17,9},{25,17},{10,2},{18,10},{26,18},{... | collective-permute-start | bytes 393224 | tf_op jit(solution)/shard_map/while/body/eval_jaxpr/ppermute | solution.py:16
  389.5 4.5 copy-start.8
  400.4 8.7 %collective-permute-start.1 = (bf16[16,4096]{1,0:T(8,128)(2,1)}, bf16[16,4096]{1,0:T(8,128)(2,1)S(1)}, u32[]{:S(2)}, u32[]{:S(2)}) collective-permute-start(bf16[16,4096]{1,0:T(8,128)(2,1)} %get-tuple-element.1274), channel_id=1, source_target_pairs={{8,0},{16,8},{24,16},{9,1},{17,9},{25,17},{10,2},{18,10},{26,18},{... | collective-permute-start | bytes 393224 | tf_op jit(solution)/shard_map/while/body/eval_jaxpr/ppermute | solution.py:16
  422.8 8.7 %collective-permute-start.1 = (bf16[16,4096]{1,0:T(8,128)(2,1)}, bf16[16,4096]{1,0:T(8,128)(2,1)S(1)}, u32[]{:S(2)}, u32[]{:S(2)}) collective-permute-start(bf16[16,4096]{1,0:T(8,128)(2,1)} %get-tuple-element.1274), channel_id=1, source_target_pairs={{8,0},{16,8},{24,16},{9,1},{17,9},{25,17},{10,2},{18,10},{26,18},{... | collective-permute-start | bytes 393224 | tf_op jit(solution)/shard_map/while/body/eval_jaxpr/ppermute | solution.py:16
  445.3 8.7 %collective-permute-start.1 = (bf16[16,4096]{1,0:T(8,128)(2,1)}, bf16[16,4096]{1,0:T(8,128)(2,1)S(1)}, u32[]{:S(2)}, u32[]{:S(2)}) collective-permute-start(bf16[16,4096]{1,0:T(8,128)(2,1)} %get-tuple-element.1274), channel_id=1, source_target_pairs={{8,0},{16,8},{24,16},{9,1},{17,9},{25,17},{10,2},{18,10},{26,18},{... | collective-permute-start | bytes 393224 | tf_op jit(solution)/shard_map/while/body/eval_jaxpr/ppermute | solution.py:16
  467.7 8.7 %collective-permute-start.1 = (bf16[16,4096]{1,0:T(8,128)(2,1)}, bf16[16,4096]{1,0:T(8,128)(2,1)S(1)}, u32[]{:S(2)}, u32[]{:S(2)}) collective-permute-start(bf16[16,4096]{1,0:T(8,128)(2,1)} %get-tuple-element.1274), channel_id=1, source_target_pairs={{8,0},{16,8},{24,16},{9,1},{17,9},{25,17},{10,2},{18,10},{26,18},{... | collective-permute-start | bytes 393224 | tf_op jit(solution)/shard_map/while/body/eval_jaxpr/ppermute | solution.py:16
  490.1 8.7 %collective-permute-start.1 = (bf16[16,4096]{1,0:T(8,128)(2,1)}, bf16[16,4096]{1,0:T(8,128)(2,1)S(1)}, u32[]{:S(2)}, u32[]{:S(2)}) collective-permute-start(bf16[16,4096]{1,0:T(8,128)(2,1)} %get-tuple-element.1274), channel_id=1, source_target_pairs={{8,0},{16,8},{24,16},{9,1},{17,9},{25,17},{10,2},{18,10},{26,18},{... | collective-permute-start | bytes 393224 | tf_op jit(solution)/shard_map/while/body/eval_jaxpr/ppermute | solution.py:16
  512.6 8.7 %collective-permute-start.1 = (bf16[16,4096]{1,0:T(8,128)(2,1)}, bf16[16,4096]{1,0:T(8,128)(2,1)S(1)}, u32[]{:S(2)}, u32[]{:S(2)}) collective-permute-start(bf16[16,4096]{1,0:T(8,128)(2,1)} %get-tuple-element.1274), channel_id=1, source_target_pairs={{8,0},{16,8},{24,16},{9,1},{17,9},{25,17},{10,2},{18,10},{26,18},{... | collective-permute-start | bytes 393224 | tf_op jit(solution)/shard_map/while/body/eval_jaxpr/ppermute | solution.py:16
  524.1 4.5 copy-start.8
  535.0 8.7 %collective-permute-start.1 = (bf16[16,4096]{1,0:T(8,128)(2,1)}, bf16[16,4096]{1,0:T(8,128)(2,1)S(1)}, u32[]{:S(2)}, u32[]{:S(2)}) collective-permute-start(bf16[16,4096]{1,0:T(8,128)(2,1)} %get-tuple-element.1274), channel_id=1, source_target_pairs={{8,0},{16,8},{24,16},{9,1},{17,9},{25,17},{10,2},{18,10},{26,18},{... | collective-permute-start | bytes 393224 | tf_op jit(solution)/shard_map/while/body/eval_jaxpr/ppermute | solution.py:16
  546.5 4.5 copy-start.8
  557.4 8.1 %collective-permute-start.1 = (bf16[16,4096]{1,0:T(8,128)(2,1)}, bf16[16,4096]{1,0:T(8,128)(2,1)S(1)}, u32[]{:S(2)}, u32[]{:S(2)}) collective-permute-start(bf16[16,4096]{1,0:T(8,128)(2,1)} %get-tuple-element.1274), channel_id=1, source_target_pairs={{8,0},{16,8},{24,16},{9,1},{17,9},{25,17},{10,2},{18,10},{26,18},{... | collective-permute-start | bytes 393224 | tf_op jit(solution)/shard_map/while/body/eval_jaxpr/ppermute | solution.py:16
  (66 other events, 191.9 us)
Sparse Core Ops, SparseCore 0:
  9.6 25.0 all-gather.8
  36.2 21.8 all-gather.10
  59.7 21.8 all-gather.12
  83.1 21.8 all-gather.14
  576.1 95.7 all-reduce.2
where the time goes:
time: 691 us; the launch traced here: 682 us
  waiting for transfers between devices  231 us (33%)
  matrix products  135 us (20%)
  local copies, waits for them, and re-layouts  130 us (19%)
  other arithmetic  124 us (18%)
  starting transfers between devices  47.5 us (7%)
  between operations  13.8 us (2%)
    psum x1, waiting for transfers between devices, on_device(): lax.psum(full_q.astype(jnp.bfloat16), 'rep').astype(jnp.float32)  96 us
    dynamic_slice x110, local copies, waits for them, and re-layouts, store_slot(): old_value = lax.dynamic_index_in_dim(store, slot_at, 0, keepdims=False)  89.3 us
    dynamic_update_slice x77, other arithmetic, store_slot(): return lax.dynamic_update_index_in_dim(store, fresh, slot_at, 0)  83.6 us
    ppermute x22, starting transfers between devices, from_behind(): return lax.ppermute(block, axis, route)  47.3 us
    ppermute x22, waiting for transfers between devices, from_behind(): return lax.ppermute(block, axis, route)  38.9 us
    all_gather x1, waiting for transfers between devices, on_device(): lax.all_gather(w_v[0], 'rep', axis=0, tiled=True)  23.5 us
    all_gather x1, waiting for transfers between devices, on_device(): lax.all_gather(w_k[0], 'rep', axis=0, tiled=True)  23.5 us
    all_gather x1, waiting for transfers between devices, on_device(): lax.all_gather(w_out[0], 'rep', axis=0, tiled=True)  23.3 us
  transfers between devices with their start and end apart: 27, of which 14 were waited for; matrix products, arithmetic and copies ran while one was open for 21% of the time, Pallas kernels for 0%

commit v1 on v0

--- a/solution.py
+++ b/solution.py
@@ -1,7 +1,12 @@
+import functools
+
 import jax
 import jax.numpy as jnp
 from jax import lax
+from jax.experimental import pallas as pl
+from jax.experimental.pallas import tpu as pltpu
 from jax.sharding import PartitionSpec as P
+
 
 MB = 8
 ROWS = 16
@@ -103,7 +108,7 @@
     )
 
 
-def on_device(x_in, cot, w_q, w_k, w_v, w_out, gains, offsets, counts):
+def pipelined(x_in, cot, w_q, w_k, w_v, w_out, gains, offsets, counts):
     section_count = lax.axis_size("section")
     rep_count = lax.axis_size("rep")
     section_pos = lax.axis_index("section")
@@ -211,6 +216,322 @@
     return (parts[0][None], parts[1][None], parts[2][None], parts[3][None])
 
 
+F32 = jnp.float32
+BF16 = jnp.bfloat16
+VMEM_LIMIT = 60 * 1024 * 1024
+
+
+def vmem_specs(count):
+    return [pl.BlockSpec(memory_space=pltpu.VMEM)] * count
+
+
+def exchange_kernel(plan, axes, *refs):
+    count = len(plan)
+    ins, outs = refs[:count], refs[count : 2 * count]
+    sems = refs[2 * count :]
+    barrier = pltpu.get_barrier_semaphore()
+    waits = 0
+    for axis, size in axes:
+        me = lax.axis_index(axis)
+        for step in range(1, size):
+            peer = lax.rem(me + step, size)
+            pl.semaphore_signal(
+                barrier, inc=1, device_id={axis: peer}, device_id_type=pl.DeviceIdType.MESH
+            )
+            waits += 1
+    pl.semaphore_wait(barrier, waits)
+    copies = []
+    for i, (axis, size, split) in enumerate(plan):
+        send, recv = sems[2 * i], sems[2 * i + 1]
+        me = lax.axis_index(axis)
+        for step in range(1, size):
+            peer = lax.rem(me + step, size)
+            copy = pltpu.make_async_remote_copy(
+                src_ref=ins[i].at[peer] if split else ins[i],
+                dst_ref=outs[i].at[me],
+                send_sem=send.at[step],
+                recv_sem=recv.at[step],
+                device_id={axis: peer},
+                device_id_type=pl.DeviceIdType.MESH,
+            )
+            copy.start()
+            copies.append((i, axis, size, split, step, copy))
+    for i, (axis, size, split) in enumerate(plan):
+        me = lax.axis_index(axis)
+        own = ins[i].at[me] if split else ins[i]
+        outs[i][me] = own[...]
+    for i, axis, size, split, step, copy in copies:
+        copy.wait_send()
+        me = lax.axis_index(axis)
+        source = lax.rem(me + size - step, size)
+        pltpu.make_async_remote_copy(
+            src_ref=outs[i].at[source],
+            dst_ref=outs[i].at[source],
+            send_sem=sems[2 * i].at[step],
+            recv_sem=sems[2 * i + 1].at[step],
+            device_id={axis: source},
+            device_id_type=pl.DeviceIdType.MESH,
+        ).wait_recv()
+
+
+def exchange(items, collective_id):
+    plan, shapes, scratch, names = [], [], [], []
+    for array, axis, split in items:
+        size = lax.axis_size(axis)
+        plan.append((axis, size, split))
+        block = array.shape[1:] if split else array.shape
+        shapes.append(jax.ShapeDtypeStruct((size,) + block, array.dtype))
+        scratch += [pltpu.SemaphoreType.DMA((size,)), pltpu.SemaphoreType.DMA((size,))]
+        if (axis, size) not in names:
+            names.append((axis, size))
+    return pl.pallas_call(
+        functools.partial(exchange_kernel, tuple(plan), tuple(names)),
+        out_shape=shapes,
+        in_specs=vmem_specs(len(items)),
+        out_specs=vmem_specs(len(items)),
+        scratch_shapes=scratch,
+        compiler_params=pltpu.CompilerParams(
+            collective_id=collective_id, has_side_effects=True, vmem_limit_bytes=VMEM_LIMIT
+        ),
+    )(*[array for array, _, _ in items])
+
+
+def dot(left, right, dims=((1,), (0,))):
+    return lax.dot_general(left, right, (dims, ((), ())), preferred_element_type=F32)
+
+
+def project_kernel(x_ref, c_ref, wt_ref, w_ref, g_ref, zx_ref, zc_ref):
+    reps, rows, shard = x_ref.shape
+    sections = w_ref.shape[0]
+    head = wt_ref.shape[0]
+    x_all = x_ref[...].reshape(reps * rows, shard)
+    c_all = c_ref[...].reshape(reps * rows, shard)
+    both = jnp.concatenate([x_all, wt_ref[...]], axis=0)
+    wide = both.astype(F32)
+
+    def put(block, at):
+        block = block.astype(BF16)
+        width = block.shape[1]
+        zx_ref[:, 0:rows, at : at + width] = block[0 : reps * rows].reshape(reps, rows, width)
+        zx_ref[:, rows:, at : at + width] = block[reps * rows :].reshape(reps, head // reps, width)
+
+    for s in range(sections):
+        at = s * 4 * head
+        scaled = (wide * g_ref[s]).astype(BF16)
+        put(dot(scaled, w_ref[s, :, 0 : 3 * head]), at)
+        w_o = w_ref[s, :, 3 * head :]
+        put(dot(both, w_o), at + 3 * head)
+        zc_ref[:, :, s * head : (s + 1) * head] = dot(c_all, w_o).astype(BF16).reshape(
+            reps, rows, head
+        )
+
+
+def chain_kernel(scale, x_ref, zx_ref, zc_ref, m_ref, keep_ref, out_ref, scal_ref):
+    sections = m_ref.shape[0]
+    head = m_ref.shape[1]
+    rows, width = x_ref.shape
+    wide = 4 * head
+    x_float = x_ref[...].astype(F32)
+    square = jnp.sum(x_float * x_float, axis=1, keepdims=True)
+    z = jnp.sum(zx_ref[:, 0:rows, :].astype(F32), axis=0)
+    back = jnp.sum(zc_ref[...].astype(F32), axis=0)
+    row = lax.broadcasted_iota(jnp.int32, (rows, rows), 0)
+    col = lax.broadcasted_iota(jnp.int32, (rows, rows), 1)
+    allowed = (row >= col) & (row // ROWS == col // ROWS)
+    y = [z[:, s * wide : s * wide + 3 * head] for s in range(sections)]
+    acto = [z[:, s * wide + 3 * head : (s + 1) * wide] for s in range(sections)]
+    saved = []
+    for s in range(sections):
+        keep = keep_ref[:, s : s + 1]
+        rinv = lax.rsqrt(jnp.maximum(square, 0.0) / width + EPSILON)
+        qkv = (y[s] * rinv).astype(BF16)
+        query, key, value = qkv[:, 0:head], qkv[:, head : 2 * head], qkv[:, 2 * head :]
+        scores = dot(query, key, ((1,), (1,))) * scale
+        expo = jnp.exp(jnp.where(allowed, scores, -1e30))
+        probs = expo / jnp.sum(expo, axis=1, keepdims=True)
+        low = probs.astype(BF16)
+        heads = dot(low, value).astype(BF16)
+        kept = heads.astype(F32) * keep
+        kept_low = kept.astype(BF16)
+        saved.append((rinv, query, key, value, probs, low, acto[:], y[s]))
+        out_ref[:, s * wide + 3 * head : (s + 1) * wide] = heads
+        moved = dot(kept_low, m_ref[s])
+        square = square + jnp.sum(
+            kept * (2.0 * acto[s] + moved[:, s * wide + 3 * head : (s + 1) * wide]),
+            axis=1,
+            keepdims=True,
+        )
+        for t in range(sections):
+            if t > s:
+                y[t] = y[t] + moved[:, t * wide : t * wide + 3 * head]
+            acto[t] = acto[t] + moved[:, t * wide + 3 * head : (t + 1) * wide]
+    bo = [back[:, s * head : (s + 1) * head] for s in range(sections)]
+    lane = lax.broadcasted_iota(jnp.int32, (rows, head), 1)
+    scal = jnp.zeros((rows, head), F32)
+    for s in range(sections - 1, -1, -1):
+        keep = keep_ref[:, s : s + 1]
+        rinv, query, key, value, probs, low, act_o, y_s = saved[s]
+        d_heads = (keep * bo[s]).astype(BF16)
+        d_value = dot(low, d_heads, ((0,), (0,))).astype(BF16)
+        d_probs = dot(d_heads, value, ((1,), (1,)))
+        d_score = (
+            probs * (d_probs - jnp.sum(probs * d_probs, axis=1, keepdims=True)) * scale
+        ).astype(BF16)
+        d_query = dot(d_score, key).astype(BF16)
+        d_key = dot(d_score, query, ((0,), (0,))).astype(BF16)
+        grads = jnp.concatenate([d_query, d_key, d_value], axis=1)
+        out_ref[:, s * wide : s * wide + 3 * head] = grads
+        mean = jnp.sum(grads.astype(F32) * y_s, axis=1, keepdims=True) / width
+        pull = rinv * rinv * rinv * mean
+        scal = jnp.where(lane == s, rinv, scal)
+        scal = jnp.where(lane == sections + s, pull, scal)
+        for t in range(s):
+            part = dot(grads, m_ref[t, :, s * wide : s * wide + 3 * head], ((1,), (1,)))
+            bo[t] = bo[t] + rinv * part - pull * act_o[t]
+    scal_ref[...] = scal
+
+
+def grads_kernel(x_ref, c_ref, made_ref, scal_ref, keep_ref, w_ref, g_ref, out_ref):
+    reps, rows, shard = x_ref.shape
+    sections = w_ref.shape[0]
+    head = w_ref.shape[2] // 4
+    wide = 4 * head
+    total = reps * rows
+    made = made_ref[...].reshape(total, sections * wide)
+    scal = scal_ref[...].reshape(total, head)
+    act = x_ref[...].reshape(total, shard).astype(F32)
+    acts = []
+    over = ((0,), (0,))
+    for s in range(sections):
+        acts.append(act)
+        rinv = scal[:, s : s + 1]
+        normed = (act * rinv * g_ref[s]).astype(BF16)
+        grads = made[:, s * wide : s * wide + 3 * head]
+        out_ref[s, :, 0 : 3 * head] = dot(normed, grads, over).astype(BF16)
+        if s + 1 < sections:
+            heads = made[:, s * wide + 3 * head : (s + 1) * wide]
+            push = dot(heads, w_ref[s, :, 3 * head :], ((1,), (1,)))
+            act = (act + keep_ref[:, s : s + 1] * push).astype(BF16).astype(F32)
+    back = c_ref[...].reshape(total, shard).astype(F32)
+    for s in range(sections - 1, -1, -1):
+        grad_rows = (keep_ref[:, s : s + 1] * back).astype(BF16)
+        heads = made[:, s * wide + 3 * head : (s + 1) * wide]
+        out_ref[s, :, 3 * head :] = dot(grad_rows, heads, over).astype(BF16)
+        if s > 0:
+            rinv = scal[:, s : s + 1]
+            pull = scal[:, sections + s : sections + s + 1]
+            grads = made[:, s * wide : s * wide + 3 * head]
+            d_normed = dot(grads, w_ref[s, :, 0 : 3 * head], ((1,), (1,)))
+            back = back + rinv * (d_normed * g_ref[s]) - pull * acts[s]
+            back = back.astype(BF16).astype(F32)
+
+
+def local_call(kernel, shapes, *arrays):
+    return pl.pallas_call(
+        kernel,
+        out_shape=shapes,
+        in_specs=vmem_specs(len(arrays)),
+        out_specs=vmem_specs(len(shapes)),
+        compiler_params=pltpu.CompilerParams(vmem_limit_bytes=VMEM_LIMIT),
+    )(*arrays)
+
+
+def low_rank(x_in, cot, w_q, w_k, w_v, w_out, gains, offsets, counts):
+    sections = lax.axis_size("section")
+    reps = lax.axis_size("rep")
+    section_pos = lax.axis_index("section")
+    rep_pos = lax.axis_index("rep")
+    width = x_in.shape[1]
+    shard, head = w_q.shape[1:]
+    batches = MB // sections
+    rows = batches * ROWS
+    wide = 4 * head
+    x_own = lax.dynamic_slice_in_dim(x_in, section_pos * rows, rows, 0)
+    c_own = lax.dynamic_slice_in_dim(cot, section_pos * rows, rows, 0)
+    x_split = x_own.reshape(rows, reps, shard).swapaxes(0, 1)
+    c_split = c_own.reshape(rows, reps, shard).swapaxes(0, 1)
+    w_pack = jnp.concatenate([w_q[0], w_k[0], w_v[0], w_out[0]], axis=1)
+    g_own = lax.dynamic_slice_in_dim(gains, rep_pos * shard, shard, 1)
+    running = jnp.zeros_like(offsets[0])
+    landed = []
+    for s in range(sections):
+        running = running + offsets[s]
+        landed.append(running % reps)
+    landed = jnp.stack(landed)
+    my_batches = lax.dynamic_slice_in_dim(landed, section_pos * batches, batches, 1)
+    rep_ids = jnp.arange(reps, dtype=jnp.int32)
+    landing = (rep_ids[None, :, None] + my_batches[:, None, :]) % reps
+    match = landing[..., None] == rep_ids
+    allowed = jnp.sum(jnp.where(match, counts[:, None, None, :], 0), axis=-1)
+    batch_ids = section_pos * batches + jnp.arange(batches, dtype=jnp.int32)
+    keep = (batch_ids < allowed).astype(F32)
+    keep = jnp.transpose(keep, (1, 2, 0))
+    keep = jnp.broadcast_to(keep[:, :, None, :], (reps, batches, ROWS, sections))
+    keep = keep.reshape(reps * rows, sections)
+    keep_own = lax.dynamic_slice_in_dim(keep, rep_pos * rows, rows, 0)
+    x_shard, c_shard, w_all, g_all = exchange(
+        [
+            (x_split, "rep", True),
+            (c_split, "rep", True),
+            (w_pack, "section", False),
+            (g_own, "section", False),
+        ],
+        0,
+    )
+    zx, zc = local_call(
+        project_kernel,
+        [
+            jax.ShapeDtypeStruct((reps, rows + head // reps, sections * wide), BF16),
+            jax.ShapeDtypeStruct((reps, rows, sections * head), BF16),
+        ],
+        x_shard,
+        c_shard,
+        w_out[0].T,
+        w_all,
+        g_all,
+    )
+    zx, zc = exchange([(zx, "rep", True), (zc, "rep", True)], 1)
+    mixed = jnp.sum(zx[:, rows:, :].astype(F32), axis=0).astype(BF16)
+    (mixed,) = exchange([(mixed, "rep", False)], 2)
+    (mixed,) = exchange([(mixed.reshape(head, sections * wide), "section", False)], 3)
+    made, scal = local_call(
+        functools.partial(chain_kernel, head ** (-0.5)),
+        [
+            jax.ShapeDtypeStruct((rows, sections * wide), BF16),
+            jax.ShapeDtypeStruct((rows, head), F32),
+        ],
+        x_own,
+        zx,
+        zc,
+        mixed,
+        keep_own,
+    )
+    made, scal = exchange([(made, "rep", False), (scal, "rep", False)], 4)
+    (parts,) = local_call(
+        grads_kernel,
+        [jax.ShapeDtypeStruct((sections, shard, wide), BF16)],
+        x_shard,
+        c_shard,
+        made,
+        scal,
+        keep,
+        w_all,
+        g_all,
+    )
+    (parts,) = exchange([(parts, "section", True)], 5)
+    total = jnp.sum(parts.astype(F32), axis=0)
+    return tuple(total[None, :, i * head : (i + 1) * head] for i in range(4))
+
+
+def on_device(*arrays):
+    sections = lax.axis_size("section")
+    head = arrays[2].shape[2]
+    reps = lax.axis_size("rep")
+    if sections <= 4 and MB % sections == 0 and head % (16 * reps) == 0:
+        return low_rank(*arrays)
+    return pipelined(*arrays)
+
+
 def solution(mesh):
     in_specs = (
         P("rep", None),

time: 691 us -> 213 us (0.31); the launches traced: 682 us -> 213 us
  waiting for transfers between devices: 231 us -> 0 us
  Pallas kernels: 0 us -> 201 us
  matrix products: 135 us -> 0 us
  local copies, waits for them, and re-layouts: 130 us -> 6.56 us
  other arithmetic: 124 us -> 4.29 us
  starting transfers between devices: 47.5 us -> 0 us
  between operations: 13.8 us -> 0.89 us
    pallas_call x0 -> x9, Pallas kernels: none -> 201 us  [the longest x6 183 us: exchange(): pl.pallas_call(functools.partial(exchange_kernel, tuple(plan), tuple(name...]
    dot_general x124 -> x0, matrix products: 135 us -> none  [the longest x8 18.7 us: forward_layer(): lax.dot_general(heads, weight_o, (((1,), (1,)), ((), ())), preferred_elem...]
    dynamic_slice x126 -> x4, local copies, waits for them, and re-layouts: 109 us -> 2.43 us  [the longest x1 1.14 us: low_rank(): c_own = lax.dynamic_slice_in_dim(cot, section_pos * rows, rows, 0)]
    psum x1 -> x0, waiting for transfers between devices: 96 us -> none  [on_device(): lax.psum(full_q.astype(jnp.bfloat16), 'rep').astype(jnp.float32)]
    all_gather x4 -> x0, waiting for transfers between devices: 93.4 us -> none  [the longest x1 23.5 us: on_device(): lax.all_gather(w_v[0], 'rep', axis=0, tiled=True)]
    dynamic_update_slice x77 -> x0, other arithmetic: 83.6 us -> none  [store_slot(): return lax.dynamic_update_index_in_dim(store, fresh, slot_at, 0)]
    ppermute x22 -> x0, starting transfers between devices: 47.3 us -> none  [from_behind(): return lax.ppermute(block, axis, route)]
    ppermute x22 -> x0, waiting for transfers between devices: 38.9 us -> none  [from_behind(): return lax.ppermute(block, axis, route)]
  transfers between devices with their start and end apart: 27 -> 0, of which waited for: 14 -> 0; matrix products, arithmetic and copies ran while one was open for 21% -> 0% of each run, Pallas kernels for 0% -> 0%
where the time goes in v1:
time: 213 us
  Pallas kernels  201 us (94%)
  local copies, waits for them, and re-layouts  6.56 us (3%)
  other arithmetic  4.29 us (2%)
    pallas_call x6, Pallas kernels, exchange(): pl.pallas_call(functools.partial(exchange_kernel, tuple(plan), tuple(name...  183 us
    pallas_call x3, Pallas kernels, local_call(): pl.pallas_call(kernel, out_shape=shapes, in_specs=vmem_specs(len(arrays))...  17.6 us

profile of v1, /device:TPU:0, one launch (start us, length us, event | category | flops | bytes accessed | tf_op | source)
XLA Modules:
  0.0 212.6 jit_solution(4990310683825108435)
XLA Ops:
  0.6 0.0 copy-start
  0.6 0.0 copy-start.4
  0.7 0.0 copy-start.5
  0.7 0.0 copy-start.6
  0.7 0.0 copy-start.7
  0.7 1.1 constant_dynamic-slice_fusion.3
  1.8 0.0 copy-start.1
  1.9 0.8 copy.38
  2.6 0.7 copy.37
  3.3 0.0 copy-done.4
  3.4 0.1 copy.30
  3.5 0.0 copy-start.2
  3.5 0.0 copy-done.5
  3.5 0.1 copy.29
  3.6 0.0 copy-done.6
  3.6 0.1 copy.28
  3.7 0.0 copy-done.7
  3.8 0.1 copy.27
  3.9 1.0 copy.31.refs_2_
  4.9 0.0 copy-done.1
  4.9 0.0 copy-done
  4.9 0.6 constant_dynamic-slice_fusion.2.refs_3_
  5.5 34.2 %shard_map.120 = (bf16[8,32,512]{2,1,0:T(8,128)(2,1)}, bf16[8,32,512]{2,1,0:T(8,128)(2,1)}, bf16[4,512,512]{2,1,0:T(8,128)(2,1)}, f32[4,1,512]{2,1,0:T(1,128)}) custom-call(bf16[8,32,512]{2,1,0:T(8,128)(2,1)} %bitcast.36, bf16[8,32,512]{2,1,0:T(8,128)(2,1)} %bitcast.37, bf16[512,512]{1,0:T(8,128)(2,1)} %copy.31.refs_2_, ...), custom_call_target="tpu_custom_call" | custom-call | tf_op jit(solution)/shard_map/pallas_call | solution.py:287
  39.8 0.0 copy-done.2
  39.8 4.6 %shard_map.121 = (bf16[8,48,2048]{2,1,0:T(8,128)(2,1)}, bf16[8,32,512]{2,1,0:T(8,128)(2,1)}) custom-call(bf16[8,32,512]{2,1,0:T(8,128)(2,1)} %get-tuple-element.16.x_ref, bf16[8,32,512]{2,1,0:T(8,128)(2,1)} %get-tuple-element.17.c_ref, bf16[128,512]{1,0:T(8,128)(2,1)} %bitcast.35, bf16[4,512,512]{2,1,0:T(8,128)(2,1)} %get-tuple-element.18.w_ref, ...), custom_call_target="tpu_custom_call" | custom-call | tf_op jit(solution)/shard_map/pallas_call | solution.py:430
  44.4 44.7 %shard_map.122 = (bf16[8,48,2048]{2,1,0:T(8,128)(2,1)}, bf16[8,32,512]{2,1,0:T(8,128)(2,1)}) custom-call(bf16[8,48,2048]{2,1,0:T(8,128)(2,1)} %get-tuple-element.20.refs_0_, bf16[8,32,512]{2,1,0:T(8,128)(2,1)} %get-tuple-element.21.refs_1_), custom_call_target="tpu_custom_call" | custom-call | tf_op jit(solution)/shard_map/pallas_call | solution.py:287
  89.1 0.0 copy-start.9
  89.1 0.0 copy-start.8
  89.1 1.8 slice_reduce_fusion.refs_0_
  90.9 13.6 %shard_map.123 = bf16[8,16,2048]{2,1,0:T(8,128)(2,1)} custom-call(bf16[16,2048]{1,0:T(8,128)(2,1)} %slice_reduce_fusion.refs_0_), custom_call_target="tpu_custom_call" | custom-call | tf_op jit(solution)/shard_map/pallas_call | solution.py:287
  104.5 28.3 %shard_map.124.m_ref = bf16[4,128,2048]{2,1,0:T(8,128)(2,1)} custom-call(bf16[128,2048]{1,0:T(8,128)(2,1)} %bitcast.33), custom_call_target="tpu_custom_call" | custom-call | tf_op jit(solution)/shard_map/pallas_call | solution.py:287
  132.8 0.0 copy-done.9
  132.8 0.1 constant_dynamic-slice_fusion.1
  132.9 0.1 and_select_fusion
  133.0 0.0 copy-done.8
  133.0 0.3 select_reduce_fusion
  133.3 0.1 fusion
  133.4 0.1 copy.32
  133.5 0.0 copy-start.3
  133.5 0.6 constant_dynamic-slice_fusion.keep_ref
  134.1 6.7 %shard_map.125 = (bf16[32,2048]{1,0:T(8,128)(2,1)}, f32[32,128]{1,0:T(8,128)}) custom-call(bf16[32,4096]{1,0:T(8,128)(2,1)} %copy-done.1, bf16[8,48,2048]{2,1,0:T(8,128)(2,1)} %get-tuple-element.22.zx_ref, bf16[8,32,512]{2,1,0:T(8,128)(2,1)} %get-tuple-element.23.zc_ref, bf16[4,128,2048]{2,1,0:T(8,128)(2,1)} %shard_map.124.m_ref, ...), custom_call_target="tpu_custom_call" | custom-call | tf_op jit(solution)/shard_map/pallas_call | solution.py:430
  140.8 0.0 copy-done.3
  140.8 33.3 %shard_map.126 = (bf16[8,32,2048]{2,1,0:T(8,128)(2,1)}, f32[8,32,128]{2,1,0:T(8,128)}) custom-call(bf16[32,2048]{1,0:T(8,128)(2,1)} %get-tuple-element.24.refs_0_, f32[32,128]{1,0:T(8,128)} %get-tuple-element.25.refs_1_), custom_call_target="tpu_custom_call" | custom-call | tf_op jit(solution)/shard_map/pallas_call | solution.py:287
  174.1 6.3 %shard_map.127.refs_0_ = bf16[4,512,512]{2,1,0:T(8,128)(2,1)} custom-call(bf16[8,32,512]{2,1,0:T(8,128)(2,1)} %get-tuple-element.16.x_ref, bf16[8,32,512]{2,1,0:T(8,128)(2,1)} %get-tuple-element.17.c_ref, bf16[8,32,2048]{2,1,0:T(8,128)(2,1)} %get-tuple-element.26.made_ref, f32[8,32,128]{2,1,0:T(8,128)} %get-tuple-element.27.scal_ref, f32[256,4]{1,0:T(8,128)} %bitcast.40, ...), custom_call_target="tpu_custom_call" | custom-call | tf_op jit(solution)/shard_map/pallas_call | solution.py:430
  180.4 29.2 %shard_map.128 = bf16[4,512,512]{2,1,0:T(8,128)(2,1)} custom-call(bf16[4,512,512]{2,1,0:T(8,128)(2,1)} %shard_map.127.refs_0_), custom_call_target="tpu_custom_call" | custom-call | tf_op jit(solution)/shard_map/pallas_call | solution.py:287
  209.6 2.0 convert_reduce_fusion
  211.6 1.0 slice_bitcast_fusion
  (5 shorter events, 0.1 us)
Async XLA Ops:
  0.6 4.3 %copy-start = (f32[1,4096]{1,0:T(1,128)S(1)}, f32[1,4096]{1,0:T(1,128)}, u32[]{:S(2)}) copy-start(f32[1,4096]{1,0:T(1,128)} %param.15) | copy-start | bytes 49156
  0.6 2.7 %copy-start.4 = (bf16[1,512,128]{2,1,0:T(8,128)(2,1)S(1)}, bf16[1,512,128]{2,1,0:T(8,128)(2,1)}, u32[]{:S(2)}) copy-start(bf16[1,512,128]{2,1,0:T(8,128)(2,1)} %param.14) | copy-start | bytes 393220
  0.7 2.8 %copy-start.5 = (bf16[1,512,128]{2,1,0:T(8,128)(2,1)S(1)}, bf16[1,512,128]{2,1,0:T(8,128)(2,1)}, u32[]{:S(2)}) copy-start(bf16[1,512,128]{2,1,0:T(8,128)(2,1)} %param.13) | copy-start | bytes 393220
  0.7 2.9 %copy-start.6 = (bf16[1,512,128]{2,1,0:T(8,128)(2,1)S(1)}, bf16[1,512,128]{2,1,0:T(8,128)(2,1)}, u32[]{:S(2)}) copy-start(bf16[1,512,128]{2,1,0:T(8,128)(2,1)} %param.12) | copy-start | bytes 393220
  0.7 3.1 %copy-start.7 = (bf16[1,512,128]{2,1,0:T(8,128)(2,1)S(1)}, bf16[1,512,128]{2,1,0:T(8,128)(2,1)}, u32[]{:S(2)}) copy-start(bf16[1,512,128]{2,1,0:T(8,128)(2,1)} %param.11) | copy-start | bytes 393220
  1.8 3.1 %copy-start.1 = (bf16[32,4096]{1,0:T(8,128)(2,1)}, bf16[32,4096]{1,0:T(8,128)(2,1)S(1)}, u32[]{:S(2)}) copy-start(bf16[32,4096]{1,0:T(8,128)(2,1)S(1)} %get-tuple-element.37.x_ref) | copy-start | bytes 786436
  3.5 36.3 %copy-start.2 = (bf16[1,512,128]{1,2,0:T(8,128)(2,1)}, bf16[1,512,128]{1,2,0:T(8,128)(2,1)S(1)}, u32[]{:S(2)}) copy-start(bf16[1,512,128]{1,2,0:T(8,128)(2,1)S(1)} %copy.30) | copy-start | bytes 393220
  89.1 43.7 %copy-start.9 = (s32[4,8]{1,0:T(4,128)S(1)}, s32[4,8]{1,0:T(4,128)}, u32[]{:S(2)}) copy-start(s32[4,8]{1,0:T(4,128)} %param.16) | copy-start | bytes 388
  89.1 43.9 %copy-start.8 = (s32[4,8]{1,0:T(4,128)S(1)}, s32[4,8]{1,0:T(4,128)}, u32[]{:S(2)}) copy-start(s32[4,8]{1,0:T(4,128)} %param.17) | copy-start | bytes 388
  133.5 7.4 %copy-start.3 = (f32[8,2,16,4]{3,2,1,0:T(8,128)}, f32[8,2,16,4]{3,2,1,0:T(8,128)S(1)}, u32[]{:S(2)}) copy-start(f32[8,2,16,4]{3,2,1,0:T(8,128)S(1)} %broadcast_in_dim.38) | copy-start | bytes 12292

commit v2 on v1

--- a/solution.py
+++ b/solution.py
@@ -225,6 +225,195 @@
     return [pl.BlockSpec(memory_space=pltpu.VMEM)] * count
 
 
+def slot(axis, index, size):
+    if axis == "rep":
+        return lax.rem(index, 2) * (size // 2) + index // 2
+    return index
+
+
+MESH_ID = pl.DeviceIdType.MESH
+
+
+def remote(src, dst, send, recv, target):
+    return pltpu.make_async_remote_copy(
+        src_ref=src, dst_ref=dst, send_sem=send, recv_sem=recv, device_id=target,
+        device_id_type=MESH_ID,
+    )
+
+
+def greet(targets):
+    barrier = pltpu.get_barrier_semaphore()
+    for target in targets:
+        pl.semaphore_signal(barrier, inc=1, device_id=target, device_id_type=MESH_ID)
+    pl.semaphore_wait(barrier, len(targets))
+
+
+def place(chips, sections):
+    rep_pos = lax.axis_index("rep")
+    core, chip = lax.rem(rep_pos, 2), rep_pos // 2
+    section = lax.axis_index("section")
+    partner = {"rep": chip * 2 + 1 - core}
+    along = []
+    for step in range(1, chips):
+        to, source = lax.rem(chip + step, chips), lax.rem(chip + chips - step, chips)
+        along.append((step, to, source, {"rep": to * 2 + core}))
+    across = []
+    for step in range(1, sections):
+        to = lax.rem(section + step, sections)
+        source = lax.rem(section + sections - step, sections)
+        across.append((step, to, source, {"section": to}))
+    return core, chip, section, partner, along, across
+
+
+def reduce_kernel(
+    z_ref, m_ref, z_land, m_out, z_core, m_core, z_sum, m_sum, m_land, m_total,
+    core_send, core_recv, z_send, z_recv, m_send, m_recv, g_send, g_recv, s_send, s_recv,
+):
+    chips, sections = z_land.shape[0], m_out.shape[1]
+    core, chip, section, partner, along, across = place(chips, sections)
+    greet([partner] + [a[3] for a in along] + [a[3] for a in across])
+    other = 1 - core
+    m_first = remote(m_ref.at[other], m_core, core_send.at[0], core_recv.at[0], partner)
+    m_first.start()
+    z_first = remote(z_ref.at[other], z_core, core_send.at[1], core_recv.at[1], partner)
+    z_first.start()
+    m_first.wait()
+    m_sum[...] = (m_ref[core].astype(F32) + m_core[...].astype(F32)).astype(BF16)
+    m_copies = []
+    for step, to, source, target in along:
+        copy = remote(m_sum.at[to], m_land.at[step], m_send.at[step], m_recv.at[step], target)
+        copy.start()
+        m_copies.append(copy)
+    total = m_sum[chip].astype(F32)
+    z_first.wait()
+    z_sum[...] = (z_ref[core].astype(F32) + z_core[...].astype(F32)).astype(BF16)
+    for copy, (step, to, source, target) in zip(m_copies, along):
+        copy.wait()
+        total = total + m_land[step].astype(F32)
+    m_total[...] = total.astype(BF16)
+    spread = []
+    for step, to, source, target in along:
+        copy = remote(
+            m_total, m_out.at[core, section, chip], g_send.at[step], g_recv.at[step], target
+        )
+        copy.start()
+        spread.append(copy)
+    z_copies = []
+    for step, to, source, target in along:
+        copy = remote(z_sum.at[to], z_land.at[step], z_send.at[step], z_recv.at[step], target)
+        copy.start()
+        z_copies.append(copy)
+    m_out[core, section, chip] = total.astype(BF16)
+    z_land[0] = z_sum[chip]
+    for copy, (step, to, source, target) in zip(spread, along):
+        copy.wait_send()
+        at = m_out.at[core, section, source]
+        remote(at, at, g_send.at[step], g_recv.at[step], target).wait_recv()
+    mine = m_out.at[core, section]
+    cross = []
+    for step, to, source, target in across:
+        copy = remote(mine, mine, s_send.at[step], s_recv.at[step], target)
+        copy.start()
+        cross.append(copy)
+    own = remote(mine, mine, core_send.at[2], core_recv.at[2], partner)
+    own.start()
+    last = []
+    for copy, (step, to, source, target) in zip(cross, across):
+        at = m_out.at[core, source]
+        remote(at, at, s_send.at[step], s_recv.at[step], target).wait_recv()
+        copy = remote(at, at, core_send.at[2 + step], core_recv.at[2 + step], partner)
+        copy.start()
+        last.append(copy)
+    for copy in z_copies:
+        copy.wait()
+    for copy in cross:
+        copy.wait_send()
+    own.wait_send()
+    at = m_out.at[other, section]
+    remote(at, at, core_send.at[2], core_recv.at[2], partner).wait_recv()
+    for copy, (step, to, source, target) in zip(last, across):
+        copy.wait_send()
+        at = m_out.at[other, source]
+        remote(at, at, core_send.at[2 + step], core_recv.at[2 + step], partner).wait_recv()
+
+
+def reduce_call(z, m, sections, collective_id):
+    two, chips = z.shape[:2]
+    block, mix = z.shape[2:], m.shape[2:]
+    dma = pltpu.SemaphoreType.DMA
+    return pl.pallas_call(
+        reduce_kernel,
+        out_shape=[
+            jax.ShapeDtypeStruct((chips,) + block, BF16),
+            jax.ShapeDtypeStruct((two, sections, chips) + mix, BF16),
+        ],
+        in_specs=vmem_specs(2),
+        out_specs=vmem_specs(2),
+        scratch_shapes=[
+            pltpu.VMEM((chips,) + block, BF16),
+            pltpu.VMEM((chips,) + mix, BF16),
+            pltpu.VMEM((chips,) + block, BF16),
+            pltpu.VMEM((chips,) + mix, BF16),
+            pltpu.VMEM((chips,) + mix, BF16),
+            pltpu.VMEM(mix, BF16),
+            dma((2 + sections,)), dma((2 + sections,)),
+            dma((chips,)), dma((chips,)), dma((chips,)), dma((chips,)),
+            dma((chips,)), dma((chips,)), dma((sections,)), dma((sections,)),
+        ],
+        compiler_params=pltpu.CompilerParams(
+            collective_id=collective_id, has_side_effects=True, vmem_limit_bytes=VMEM_LIMIT
+        ),
+    )(z, m)
+
+
+def gather_kernel(a_ref, b_ref, a_out, b_out, core_send, core_recv, z_send, z_recv):
+    chips = a_out.shape[1]
+    core, chip, section, partner, along, across = place(chips, 1)
+    greet([partner] + [a[3] for a in along])
+    other = 1 - core
+    outs = ((a_ref, a_out), (b_ref, b_out))
+    sends = []
+    for step, to, source, target in along:
+        for i, (ref, out) in enumerate(outs):
+            copy = remote(
+                ref, out.at[core, chip], z_send.at[i, step], z_recv.at[i, step], target
+            )
+            copy.start()
+            sends.append(copy)
+    for i, (ref, out) in enumerate(outs):
+        copy = remote(ref, out.at[core, chip], core_send.at[i, 0], core_recv.at[i, 0], partner)
+        copy.start()
+        sends.append(copy)
+        out[core, chip] = ref[...]
+    for step, to, source, target in along:
+        for i, (ref, out) in enumerate(outs):
+            at = out.at[core, source]
+            remote(at, at, z_send.at[i, step], z_recv.at[i, step], target).wait_recv()
+            copy = remote(at, at, core_send.at[i, step], core_recv.at[i, step], partner)
+            copy.start()
+            sends.append(copy)
+    for copy in sends:
+        copy.wait_send()
+    for step, source in [(0, chip)] + [(a[0], a[2]) for a in along]:
+        for i, (ref, out) in enumerate(outs):
+            at = out.at[other, source]
+            remote(at, at, core_send.at[i, step], core_recv.at[i, step], partner).wait_recv()
+
+
+def gather_call(a, b, chips, collective_id):
+    dma = pltpu.SemaphoreType.DMA
+    return pl.pallas_call(
+        gather_kernel,
+        out_shape=[jax.ShapeDtypeStruct((2, chips) + v.shape, v.dtype) for v in (a, b)],
+        in_specs=vmem_specs(2),
+        out_specs=vmem_specs(2),
+        scratch_shapes=[dma((2, chips)) for _ in range(4)],
+        compiler_params=pltpu.CompilerParams(
+            collective_id=collective_id, has_side_effects=True, vmem_limit_bytes=VMEM_LIMIT
+        ),
+    )(a, b)
+
+
 def exchange_kernel(plan, axes, *refs):
     count = len(plan)
     ins, outs = refs[:count], refs[count : 2 * count]
@@ -248,7 +437,7 @@
             peer = lax.rem(me + step, size)
             copy = pltpu.make_async_remote_copy(
                 src_ref=ins[i].at[peer] if split else ins[i],
-                dst_ref=outs[i].at[me],
+                dst_ref=outs[i].at[slot(axis, me, size)],
                 send_sem=send.at[step],
                 recv_sem=recv.at[step],
                 device_id={axis: peer},
@@ -259,14 +448,15 @@
     for i, (axis, size, split) in enumerate(plan):
         me = lax.axis_index(axis)
         own = ins[i].at[me] if split else ins[i]
-        outs[i][me] = own[...]
+        outs[i][slot(axis, me, size)] = own[...]
     for i, axis, size, split, step, copy in copies:
         copy.wait_send()
         me = lax.axis_index(axis)
         source = lax.rem(me + size - step, size)
+        at = slot(axis, source, size)
         pltpu.make_async_remote_copy(
-            src_ref=outs[i].at[source],
-            dst_ref=outs[i].at[source],
+            src_ref=outs[i].at[at],
+            dst_ref=outs[i].at[at],
             send_sem=sems[2 * i].at[step],
             recv_sem=sems[2 * i + 1].at[step],
             device_id={axis: source},
@@ -300,41 +490,59 @@
     return lax.dot_general(left, right, (dims, ((), ())), preferred_element_type=F32)
 
 
-def project_kernel(x_ref, c_ref, wt_ref, w_ref, g_ref, zx_ref, zc_ref):
+def project_kernel(x_ref, c_ref, w_ref, g_ref, z_ref, m_ref):
     reps, rows, shard = x_ref.shape
     sections = w_ref.shape[0]
-    head = wt_ref.shape[0]
+    head = w_ref.shape[2] // 4
+    qkv = 3 * head
+    me = lax.axis_index("section")
     x_all = x_ref[...].reshape(reps * rows, shard)
     c_all = c_ref[...].reshape(reps * rows, shard)
-    both = jnp.concatenate([x_all, wt_ref[...]], axis=0)
-    wide = both.astype(F32)
-
-    def put(block, at):
-        block = block.astype(BF16)
-        width = block.shape[1]
-        zx_ref[:, 0:rows, at : at + width] = block[0 : reps * rows].reshape(reps, rows, width)
-        zx_ref[:, rows:, at : at + width] = block[reps * rows :].reshape(reps, head // reps, width)
-
+    wide = x_all.astype(F32)
+
+    def put(ref, at, block):
+        shape = ref.shape[:3] + (block.shape[1],)
+        ref[:, :, :, at : at + block.shape[1]] = block.astype(BF16).reshape(shape)
+
+    for gap in range(1, sections // 2 + 1):
+        far = lax.rem(me + gap, sections)
+        low, high = jnp.minimum(me, far), jnp.maximum(me, far)
+        turned = jnp.transpose(w_ref[low, :, qkv:].astype(F32))
+        turned = (turned * g_ref[high]).astype(BF16)
+        put(m_ref, (gap - 1) * qkv, dot(turned, w_ref[high, :, 0:qkv]))
+    w_me = w_ref[me, :, qkv:]
+    base = sections // 2 * qkv
     for s in range(sections):
-        at = s * 4 * head
         scaled = (wide * g_ref[s]).astype(BF16)
-        put(dot(scaled, w_ref[s, :, 0 : 3 * head]), at)
-        w_o = w_ref[s, :, 3 * head :]
-        put(dot(both, w_o), at + 3 * head)
-        zc_ref[:, :, s * head : (s + 1) * head] = dot(c_all, w_o).astype(BF16).reshape(
-            reps, rows, head
-        )
-
-
-def chain_kernel(scale, x_ref, zx_ref, zc_ref, m_ref, keep_ref, out_ref, scal_ref):
-    sections = m_ref.shape[0]
-    head = m_ref.shape[1]
+        w_o = w_ref[s, :, qkv:]
+        put(z_ref, s * 4 * head, dot(scaled, w_ref[s, :, 0:qkv]))
+        put(z_ref, s * 4 * head + qkv, dot(x_all, w_o))
+        put(z_ref, (sections * 4 + s) * head, dot(c_all, w_o))
+        put(m_ref, base + s * head, dot(w_me, w_o, ((0,), (0,))))
+
+
+def chain_kernel(scale, x_ref, z_ref, m_ref, keep_ref, out_ref, scal_ref):
+    sections = keep_ref.shape[1]
+    head = scal_ref.shape[1]
     rows, width = x_ref.shape
     wide = 4 * head
     x_float = x_ref[...].astype(F32)
     square = jnp.sum(x_float * x_float, axis=1, keepdims=True)
-    z = jnp.sum(zx_ref[:, 0:rows, :].astype(F32), axis=0)
-    back = jnp.sum(zc_ref[...].astype(F32), axis=0)
+    z = jnp.sum(z_ref[...].astype(F32), axis=0)
+    back = z[:, sections * wide :]
+    base = sections // 2 * 3 * head
+    mix = [
+        jnp.concatenate([m_ref[c, s].reshape(head // 2, -1) for c in range(2)], axis=0)
+        for s in range(sections)
+    ]
+
+    def pair(low, high):
+        gap = high - low
+        owner = low
+        if gap > sections // 2:
+            owner, gap = high, sections - gap
+        return mix[owner][:, (gap - 1) * 3 * head : gap * 3 * head]
+
     row = lax.broadcasted_iota(jnp.int32, (rows, rows), 0)
     col = lax.broadcasted_iota(jnp.int32, (rows, rows), 1)
     allowed = (row >= col) & (row // ROWS == col // ROWS)
@@ -355,16 +563,16 @@
         kept_low = kept.astype(BF16)
         saved.append((rinv, query, key, value, probs, low, acto[:], y[s]))
         out_ref[:, s * wide + 3 * head : (s + 1) * wide] = heads
-        moved = dot(kept_low, m_ref[s])
+        moved = dot(kept_low, mix[s][:, base:])
         square = square + jnp.sum(
-            kept * (2.0 * acto[s] + moved[:, s * wide + 3 * head : (s + 1) * wide]),
+            kept * (2.0 * acto[s] + moved[:, s * head : (s + 1) * head]),
             axis=1,
             keepdims=True,
         )
         for t in range(sections):
             if t > s:
-                y[t] = y[t] + moved[:, t * wide : t * wide + 3 * head]
-            acto[t] = acto[t] + moved[:, t * wide + 3 * head : (t + 1) * wide]
+                y[t] = y[t] + dot(kept_low, pair(s, t))
+            acto[t] = acto[t] + moved[:, t * head : (t + 1) * head]
     bo = [back[:, s * head : (s + 1) * head] for s in range(sections)]
     lane = lax.broadcasted_iota(jnp.int32, (rows, head), 1)
     scal = jnp.zeros((rows, head), F32)
@@ -386,7 +594,7 @@
         scal = jnp.where(lane == s, rinv, scal)
         scal = jnp.where(lane == sections + s, pull, scal)
         for t in range(s):
-            part = dot(grads, m_ref[t, :, s * wide : s * wide + 3 * head], ((1,), (1,)))
+            part = dot(grads, pair(t, s), ((1,), (1,)))
             bo[t] = bo[t] + rinv * part - pull * act_o[t]
     scal_ref[...] = scal
 
@@ -444,6 +652,7 @@
     width = x_in.shape[1]
     shard, head = w_q.shape[1:]
     batches = MB // sections
+    chips = reps // 2
     rows = batches * ROWS
     wide = 4 * head
     x_own = lax.dynamic_slice_in_dim(x_in, section_pos * rows, rows, 0)
@@ -460,7 +669,8 @@
     landed = jnp.stack(landed)
     my_batches = lax.dynamic_slice_in_dim(landed, section_pos * batches, batches, 1)
     rep_ids = jnp.arange(reps, dtype=jnp.int32)
-    landing = (rep_ids[None, :, None] + my_batches[:, None, :]) % reps
+    slots = (rep_ids % chips) * 2 + rep_ids // chips
+    landing = (slots[None, :, None] + my_batches[:, None, :]) % reps
     match = landing[..., None] == rep_ids
     allowed = jnp.sum(jnp.where(match, counts[:, None, None, :], 0), axis=-1)
     batch_ids = section_pos * batches + jnp.arange(batches, dtype=jnp.int32)
@@ -468,7 +678,7 @@
     keep = jnp.transpose(keep, (1, 2, 0))
     keep = jnp.broadcast_to(keep[:, :, None, :], (reps, batches, ROWS, sections))
     keep = keep.reshape(reps * rows, sections)
-    keep_own = lax.dynamic_slice_in_dim(keep, rep_pos * rows, rows, 0)
+    keep_own = lax.dynamic_slice_in_dim(keep, slot("rep", rep_pos, reps) * rows, rows, 0)
     x_shard, c_shard, w_all, g_all = exchange(
         [
             (x_split, "rep", True),
@@ -478,22 +688,19 @@
         ],
         0,
     )
-    zx, zc = local_call(
+    mix_width = sections // 2 * 3 * head + sections * head
+    z, mixed = local_call(
         project_kernel,
         [
-            jax.ShapeDtypeStruct((reps, rows + head // reps, sections * wide), BF16),
-            jax.ShapeDtypeStruct((reps, rows, sections * head), BF16),
+            jax.ShapeDtypeStruct((2, chips, rows, sections * 5 * head), BF16),
+            jax.ShapeDtypeStruct((2, chips, head // reps, mix_width), BF16),
         ],
         x_shard,
         c_shard,
-        w_out[0].T,
         w_all,
         g_all,
     )
-    zx, zc = exchange([(zx, "rep", True), (zc, "rep", True)], 1)
-    mixed = jnp.sum(zx[:, rows:, :].astype(F32), axis=0).astype(BF16)
-    (mixed,) = exchange([(mixed, "rep", False)], 2)
-    (mixed,) = exchange([(mixed.reshape(head, sections * wide), "section", False)], 3)
+    z, mixed = reduce_call(z, mixed, sections, 1)
     made, scal = local_call(
         functools.partial(chain_kernel, head ** (-0.5)),
         [
@@ -501,12 +708,11 @@
             jax.ShapeDtypeStruct((rows, head), F32),
         ],
         x_own,
-        zx,
-        zc,
+        z,
         mixed,
         keep_own,
     )
-    made, scal = exchange([(made, "rep", False), (scal, "rep", False)], 4)
+    made, scal = gather_call(made, scal, chips, 2)
     (parts,) = local_call(
         grads_kernel,
         [jax.ShapeDtypeStruct((sections, shard, wide), BF16)],
@@ -518,7 +724,7 @@
         w_all,
         g_all,
     )
-    (parts,) = exchange([(parts, "section", True)], 5)
+    (parts,) = exchange([(parts, "section", True)], 3)
     total = jnp.sum(parts.astype(F32), axis=0)
     return tuple(total[None, :, i * head : (i + 1) * head] for i in range(4))
 
@@ -527,7 +733,7 @@
     sections = lax.axis_size("section")
     head = arrays[2].shape[2]
     reps = lax.axis_size("rep")
-    if sections <= 4 and MB % sections == 0 and head % (16 * reps) == 0:
+    if sections == 4 and reps % 2 == 0 and head % (16 * reps) == 0:
         return low_rank(*arrays)
     return pipelined(*arrays)
 

time: 213 us -> 138 us (0.65)
  Pallas kernels: 201 us -> 128 us
    pallas_call x6 -> x2, Pallas kernels: 183 us -> 63.7 us  [exchange(): pl.pallas_call(functools.partial(exchange_kernel, tuple(plan), tuple(name...]
    pallas_call x0 -> x2, Pallas kernels: none -> 47.4 us  [the longest x1 28 us: reduce_call(): pl.pallas_call(reduce_kernel, out_shape=[jax.ShapeDtypeStruct((chips,) +...]
where the time goes in v2:
time: 138 us
  Pallas kernels  128 us (93%)
  local copies, waits for them, and re-layouts  5.68 us (4%)
  other arithmetic  3.35 us (2%)
    pallas_call x2, Pallas kernels, exchange(): pl.pallas_call(functools.partial(exchange_kernel, tuple(plan), tuple(name...  63.7 us
    pallas_call x1, Pallas kernels, reduce_call(): pl.pallas_call(reduce_kernel, out_shape=[jax.ShapeDtypeStruct((chips,) +...  28 us
    pallas_call x1, Pallas kernels, gather_call(): pl.pallas_call(gather_kernel, out_shape=[jax.ShapeDtypeStruct((2, chips)...  19.4 us
    pallas_call x3, Pallas kernels, local_call(): pl.pallas_call(kernel, out_shape=shapes, in_specs=vmem_specs(len(arrays))...  17 us

profile of v2, /device:TPU:0, one launch (start us, length us, event | category | flops | bytes accessed | tf_op | source)
XLA Modules:
  0.0 138.0 jit_solution(3240700311418177280)
XLA Ops:
  0.6 0.0 copy-start
  0.6 0.0 copy-start.6
  0.7 0.0 copy-start.5
  0.7 0.0 copy-start.4
  0.7 0.0 copy-start.3
  0.7 0.7 copy-done
  1.4 0.6 constant_dynamic-slice_fusion.2.refs_3_
  1.9 1.1 constant_dynamic-slice_fusion.3
  3.0 0.0 copy-start.1
  3.0 0.8 copy.23
  3.8 0.7 copy.22
  4.5 0.0 copy-done.6
  4.5 0.0 copy-done.5
  4.5 0.0 copy-done.4
  4.5 0.0 copy-done.3
  4.5 0.9 pad_maximum_fusion.refs_2_
  5.4 34.2 %shard_map.120 = (bf16[8,32,512]{2,1,0:T(8,128)(2,1)}, bf16[8,32,512]{2,1,0:T(8,128)(2,1)}, bf16[4,512,512]{2,1,0:T(8,128)(2,1)}, f32[4,1,512]{2,1,0:T(1,128)}) custom-call(bf16[8,32,512]{2,1,0:T(8,128)(2,1)} %bitcast.30, bf16[8,32,512]{2,1,0:T(8,128)(2,1)} %bitcast.31, bf16[512,512]{1,0:T(8,128)(2,1)} %pad_maximum_fusion.refs_2_, ...), custom_call_target="tpu_custom_call" | custom-call | tf_op jit(solution)/shard_map/pallas_call | solution.py:477
  39.6 0.0 copy-start.8
  39.6 0.0 copy-start.7
  39.6 4.5 %shard_map.121 = (bf16[2,4,32,2560]{3,2,1,0:T(8,128)(2,1)}, bf16[2,4,16,1280]{3,2,1,0:T(8,128)(2,1)}) custom-call(bf16[8,32,512]{2,1,0:T(8,128)(2,1)} %get-tuple-element.16.x_ref, bf16[8,32,512]{2,1,0:T(8,128)(2,1)} %get-tuple-element.17.c_ref, bf16[4,512,512]{2,1,0:T(8,128)(2,1)} %get-tuple-element.18.w_ref, f32[4,1,512]{2,1,0:T(1,128)} %get-tuple-element.19.g_ref), custom_call_target="tpu_custom_call" | custom-call | tf_op jit(solution)/shard_map/pallas_call | solution.py:638
  44.1 0.0 copy-done.1
  44.1 28.0 %shard_map.122 = (bf16[4,32,2560]{2,1,0:T(8,128)(2,1)}, bf16[2,4,4,16,1280]{4,3,2,1,0:T(8,128)(2,1)}) custom-call(bf16[2,4,32,2560]{3,2,1,0:T(8,128)(2,1)} %get-tuple-element.20.z_ref, bf16[2,4,16,1280]{3,2,1,0:T(8,128)(2,1)} %get-tuple-element.21.m_ref), custom_call_target="tpu_custom_call" | custom-call | tf_op jit(solution)/shard_map/pallas_call | solution.py:344
  72.1 0.0 copy-done.8
  72.2 0.1 constant_dynamic-slice_fusion.1
  72.3 0.1 and_select_fusion
  72.4 0.0 copy-done.7
  72.4 0.3 select_reduce_fusion
  72.7 0.1 fusion.1
  72.7 0.1 copy.17
  72.9 0.0 copy-start.2
  72.9 0.6 constant_dynamic-slice_fusion.keep_ref
  73.5 6.2 %shard_map.123 = (bf16[32,2048]{1,0:T(8,128)(2,1)}, f32[32,128]{1,0:T(8,128)}) custom-call(bf16[32,4096]{1,0:T(8,128)(2,1)} %copy-done.1, bf16[4,32,2560]{2,1,0:T(8,128)(2,1)} %get-tuple-element.22.z_ref, bf16[2,4,4,16,1280]{4,3,2,1,0:T(8,128)(2,1)} %get-tuple-element.23.m_ref, f32[32,4]{1,0:T(8,128)} %constant_dynamic-slice_fusion.keep_ref), custom_call_target="tpu_custom_call" | custom-call | tf_op jit(solution)/shard_map/pallas_call | solution.py:638
  79.7 19.4 %shard_map.124 = (bf16[2,4,32,2048]{3,2,1,0:T(8,128)(2,1)}, f32[2,4,32,128]{3,2,1,0:T(8,128)}) custom-call(bf16[32,2048]{1,0:T(8,128)(2,1)} %get-tuple-element.24.a_ref, f32[32,128]{1,0:T(8,128)} %get-tuple-element.25.b_ref), custom_call_target="tpu_custom_call" | custom-call | tf_op jit(solution)/shard_map/pallas_call | solution.py:405
  99.1 0.0 copy-done.2
  99.1 6.3 %shard_map.125.refs_0_ = bf16[4,512,512]{2,1,0:T(8,128)(2,1)} custom-call(bf16[8,32,512]{2,1,0:T(8,128)(2,1)} %get-tuple-element.16.x_ref, bf16[8,32,512]{2,1,0:T(8,128)(2,1)} %get-tuple-element.17.c_ref, bf16[2,4,32,2048]{3,2,1,0:T(8,128)(2,1)} %get-tuple-element.26.made_ref, f32[2,4,32,128]{3,2,1,0:T(8,128)} %get-tuple-element.27.scal_ref, ...), custom_call_target="tpu_custom_call" | custom-call | tf_op jit(solution)/shard_map/pallas_call | solution.py:638
  105.4 29.5 %shard_map.126 = bf16[4,512,512]{2,1,0:T(8,128)(2,1)} custom-call(bf16[4,512,512]{2,1,0:T(8,128)(2,1)} %shard_map.125.refs_0_), custom_call_target="tpu_custom_call" | custom-call | tf_op jit(solution)/shard_map/pallas_call | solution.py:477
  134.9 2.0 %convert_reduce_fusion = f32[512,512]{1,0:T(8,128)S(1)} fusion(bf16[4,512,512]{2,1,0:T(8,128)(2,1)} %shard_map.126), kind=kLoop, calls=%fused_computation | loop fusion | flops 1835008 | bytes 3145728 | tf_op jit(solution)/shard_map/reduce_sum | solution.py:728
  137.0 1.0 slice_bitcast_fusion
  (5 shorter events, 0.1 us)
Async XLA Ops:
  0.6 0.7 copy-start
  0.6 3.9 %copy-start.6 = (bf16[1,512,128]{2,1,0:T(8,128)(2,1)S(1)}, bf16[1,512,128]{2,1,0:T(8,128)(2,1)}, u32[]{:S(2)}) copy-start(bf16[1,512,128]{2,1,0:T(8,128)(2,1)} %param.11) | copy-start | bytes 393220
  0.7 3.9 %copy-start.5 = (bf16[1,512,128]{2,1,0:T(8,128)(2,1)S(1)}, bf16[1,512,128]{2,1,0:T(8,128)(2,1)}, u32[]{:S(2)}) copy-start(bf16[1,512,128]{2,1,0:T(8,128)(2,1)} %param.12) | copy-start | bytes 393220
  0.7 3.9 %copy-start.4 = (bf16[1,512,128]{2,1,0:T(8,128)(2,1)S(1)}, bf16[1,512,128]{2,1,0:T(8,128)(2,1)}, u32[]{:S(2)}) copy-start(bf16[1,512,128]{2,1,0:T(8,128)(2,1)} %param.13) | copy-start | bytes 393220
  0.7 3.9 %copy-start.3 = (bf16[1,512,128]{2,1,0:T(8,128)(2,1)S(1)}, bf16[1,512,128]{2,1,0:T(8,128)(2,1)}, u32[]{:S(2)}) copy-start(bf16[1,512,128]{2,1,0:T(8,128)(2,1)} %param.14) | copy-start | bytes 393220
  3.0 41.1 %copy-start.1 = (bf16[32,4096]{1,0:T(8,128)(2,1)}, bf16[32,4096]{1,0:T(8,128)(2,1)S(1)}, u32[]{:S(2)}) copy-start(bf16[32,4096]{1,0:T(8,128)(2,1)S(1)} %get-tuple-element.37.x_ref) | copy-start | bytes 786436
  39.6 32.5 %copy-start.8 = (s32[4,8]{1,0:T(4,128)S(1)}, s32[4,8]{1,0:T(4,128)}, u32[]{:S(2)}) copy-start(s32[4,8]{1,0:T(4,128)} %param.16) | copy-start | bytes 388
  39.6 32.7 %copy-start.7 = (s32[4,8]{1,0:T(4,128)S(1)}, s32[4,8]{1,0:T(4,128)}, u32[]{:S(2)}) copy-start(s32[4,8]{1,0:T(4,128)} %param.17) | copy-start | bytes 388
  72.9 26.2 %copy-start.2 = (f32[8,2,16,4]{3,2,1,0:T(8,128)}, f32[8,2,16,4]{3,2,1,0:T(8,128)S(1)}, u32[]{:S(2)}) copy-start(f32[8,2,16,4]{3,2,1,0:T(8,128)S(1)} %broadcast_in_dim.38) | copy-start | bytes 12292

commit v3 on v2

--- a/solution.py
+++ b/solution.py
@@ -366,54 +366,6 @@
     )(z, m)
 
 
-def gather_kernel(a_ref, b_ref, a_out, b_out, core_send, core_recv, z_send, z_recv):
-    chips = a_out.shape[1]
-    core, chip, section, partner, along, across = place(chips, 1)
-    greet([partner] + [a[3] for a in along])
-    other = 1 - core
-    outs = ((a_ref, a_out), (b_ref, b_out))
-    sends = []
-    for step, to, source, target in along:
-        for i, (ref, out) in enumerate(outs):
-            copy = remote(
-                ref, out.at[core, chip], z_send.at[i, step], z_recv.at[i, step], target
-            )
-            copy.start()
-            sends.append(copy)
-    for i, (ref, out) in enumerate(outs):
-        copy = remote(ref, out.at[core, chip], core_send.at[i, 0], core_recv.at[i, 0], partner)
-        copy.start()
-        sends.append(copy)
-        out[core, chip] = ref[...]
-    for step, to, source, target in along:
-        for i, (ref, out) in enumerate(outs):
-            at = out.at[core, source]
-            remote(at, at, z_send.at[i, step], z_recv.at[i, step], target).wait_recv()
-            copy = remote(at, at, core_send.at[i, step], core_recv.at[i, step], partner)
-            copy.start()
-            sends.append(copy)
-    for copy in sends:
-        copy.wait_send()
-    for step, source in [(0, chip)] + [(a[0], a[2]) for a in along]:
-        for i, (ref, out) in enumerate(outs):
-            at = out.at[other, source]
-            remote(at, at, core_send.at[i, step], core_recv.at[i, step], partner).wait_recv()
-
-
-def gather_call(a, b, chips, collective_id):
-    dma = pltpu.SemaphoreType.DMA
-    return pl.pallas_call(
-        gather_kernel,
-        out_shape=[jax.ShapeDtypeStruct((2, chips) + v.shape, v.dtype) for v in (a, b)],
-        in_specs=vmem_specs(2),
-        out_specs=vmem_specs(2),
-        scratch_shapes=[dma((2, chips)) for _ in range(4)],
-        compiler_params=pltpu.CompilerParams(
-            collective_id=collective_id, has_side_effects=True, vmem_limit_bytes=VMEM_LIMIT
-        ),
-    )(a, b)
-
-
 def exchange_kernel(plan, axes, *refs):
     count = len(plan)
     ins, outs = refs[:count], refs[count : 2 * count]
@@ -562,7 +514,7 @@
         kept = heads.astype(F32) * keep
         kept_low = kept.astype(BF16)
         saved.append((rinv, query, key, value, probs, low, acto[:], y[s]))
-        out_ref[:, s * wide + 3 * head : (s + 1) * wide] = heads
+        out_ref[0, :, s * head : (s + 1) * head] = heads
         moved = dot(kept_low, mix[s][:, base:])
         square = square + jnp.sum(
             kept * (2.0 * acto[s] + moved[:, s * head : (s + 1) * head]),
@@ -588,7 +540,9 @@
         d_query = dot(d_score, key).astype(BF16)
         d_key = dot(d_score, query, ((0,), (0,))).astype(BF16)
         grads = jnp.concatenate([d_query, d_key, d_value], axis=1)
-        out_ref[:, s * wide : s * wide + 3 * head] = grads
+        out_ref[1, :, s * head : (s + 1) * head] = d_value
+        out_ref[2, :, s * head : (s + 1) * head] = d_query
+        out_ref[3, :, s * head : (s + 1) * head] = d_key
         mean = jnp.sum(grads.astype(F32) * y_s, axis=1, keepdims=True) / width
         pull = rinv * rinv * rinv * mean
         scal = jnp.where(lane == s, rinv, scal)
@@ -599,39 +553,179 @@
     scal_ref[...] = scal
 
 
-def grads_kernel(x_ref, c_ref, made_ref, scal_ref, keep_ref, w_ref, g_ref, out_ref):
+def tail_kernel(
+    x_ref, c_ref, made_ref, scal_ref, keep_ref, w_ref, g_ref,
+    q_out, k_out, v_out, o_out,
+    made, scal, normed, acts, part, relay, from_x, from_y, merged,
+    z_send, z_recv, core_send, core_recv, h_send, h_recv,
+):
     reps, rows, shard = x_ref.shape
     sections = w_ref.shape[0]
     head = w_ref.shape[2] // 4
-    wide = 4 * head
+    qkv = 3 * head
+    half = shard // 2
+    chips = reps // 2
     total = reps * rows
-    made = made_ref[...].reshape(total, sections * wide)
-    scal = scal_ref[...].reshape(total, head)
+    core, chip, section, partner, along, _ = place(chips, 1)
+    other = 1 - core
+    near_x = section + 1 - 2 * lax.rem(section, 2)
+    near_y = lax.rem(section + 2, 4)
+    diagonal = 3 - section
+    to_x, to_y = {"section": near_x}, {"section": near_y}
+    greet([partner] + [a[3] for a in along] + [to_x, to_y])
+    outs = [made.at[i] for i in range(4)] + [scal]
+    ins = [made_ref.at[i] for i in range(4)] + [scal_ref]
+    sends = []
+
+    def start(copy):
+        copy.start()
+        sends.append(copy)
+
+    for i in (4, 0, 1, 2, 3):
+        for step, to, source, target in along:
+            at = outs[i].at[core, chip]
+            start(remote(ins[i], at, z_send.at[i, step], z_recv.at[i, step], target))
+        at = outs[i].at[core, chip]
+        start(remote(ins[i], at, core_send.at[i, 0], core_recv.at[i, 0], partner))
+    for i in range(4):
+        made[i, core, chip] = made_ref[i]
+    scal[core, chip] = scal_ref[...]
+
+    def arrive(kinds):
+        for i in kinds:
+            for step, to, source, target in along:
+                at = outs[i].at[core, source]
+                remote(at, at, z_send.at[i, step], z_recv.at[i, step], target).wait_recv()
+                start(remote(at, at, core_send.at[i, step], core_recv.at[i, step], partner))
+        for i in kinds:
+            for step, source in [(0, chip)] + [(a[0], a[2]) for a in along]:
+                at = outs[i].at[other, source]
+                remote(at, at, core_send.at[i, step], core_recv.at[i, step], partner).wait_recv()
+
+    first, second = pl.ds(0, half), pl.ds(half, half)
+
+    def message(kind, number, src, dst, target):
+        return remote(src, dst, h_send.at[kind, number], h_recv.at[kind, number], target)
+
+    def messages(kind):
+        p = part.at[kind]
+        return [
+            message(kind, 0, p.at[diagonal, first], relay.at[kind, 0], to_x),
+            message(kind, 1, p.at[near_x, first], from_x.at[kind, first], to_x),
+            message(kind, 2, merged.at[kind, 1], from_x.at[kind, second], to_x),
+            message(kind, 3, p.at[diagonal, second], relay.at[kind, 1], to_y),
+            message(kind, 4, p.at[near_y, second], from_y.at[kind, second], to_y),
+            message(kind, 5, merged.at[kind, 0], from_y.at[kind, first], to_y),
+        ]
+
+    def send_parts(kind):
+        copies = messages(kind)
+        for number in (0, 3, 1, 4):
+            start(copies[number])
+
+    def send_merged(kind):
+        copies = messages(kind)
+        copies[0].wait_recv()
+        merged[kind, 0] = (
+            relay[kind, 0].astype(F32) + part[kind, near_y, 0:half].astype(F32)
+        ).astype(BF16)
+        start(copies[5])
+        copies[3].wait_recv()
+        merged[kind, 1] = (
+            relay[kind, 1].astype(F32) + part[kind, near_x, half:].astype(F32)
+        ).astype(BF16)
+        start(copies[2])
+
+    def block(kind, s):
+        return made[kind, :, :, :, s * head : (s + 1) * head].reshape(total, head)
+
+    def column(at):
+        return scal[:, :, :, at : at + 1].reshape(total, 1)
+
+    over = ((0,), (0,))
+    across = ((1,), (1,))
+    arrive((4, 0, 1))
     act = x_ref[...].reshape(total, shard).astype(F32)
-    acts = []
-    over = ((0,), (0,))
     for s in range(sections):
-        acts.append(act)
-        rinv = scal[:, s : s + 1]
-        normed = (act * rinv * g_ref[s]).astype(BF16)
-        grads = made[:, s * wide : s * wide + 3 * head]
-        out_ref[s, :, 0 : 3 * head] = dot(normed, grads, over).astype(BF16)
+        acts[s] = act.astype(BF16)
+        normed[s] = (act * column(s) * g_ref[s]).astype(BF16)
+        part[2, s] = dot(normed[s], block(1, s), over).astype(BF16)
         if s + 1 < sections:
-            heads = made[:, s * wide + 3 * head : (s + 1) * wide]
-            push = dot(heads, w_ref[s, :, 3 * head :], ((1,), (1,)))
+            push = dot(block(0, s), w_ref[s, :, qkv:], across)
             act = (act + keep_ref[:, s : s + 1] * push).astype(BF16).astype(F32)
+    send_parts(2)
+    arrive((2,))
+    for s in range(sections):
+        part[0, s] = dot(normed[s], block(2, s), over).astype(BF16)
+    send_parts(0)
+    arrive((3,))
+    for s in range(sections):
+        part[1, s] = dot(normed[s], block(3, s), over).astype(BF16)
+    send_merged(2)
+    send_parts(1)
     back = c_ref[...].reshape(total, shard).astype(F32)
     for s in range(sections - 1, -1, -1):
         grad_rows = (keep_ref[:, s : s + 1] * back).astype(BF16)
-        heads = made[:, s * wide + 3 * head : (s + 1) * wide]
-        out_ref[s, :, 3 * head :] = dot(grad_rows, heads, over).astype(BF16)
+        part[3, s] = dot(grad_rows, block(0, s), over).astype(BF16)
         if s > 0:
-            rinv = scal[:, s : s + 1]
-            pull = scal[:, sections + s : sections + s + 1]
-            grads = made[:, s * wide : s * wide + 3 * head]
-            d_normed = dot(grads, w_ref[s, :, 0 : 3 * head], ((1,), (1,)))
-            back = back + rinv * (d_normed * g_ref[s]) - pull * acts[s]
+            d_normed = dot(block(2, s), w_ref[s, :, 0:head], across)
+            d_normed = d_normed + dot(block(3, s), w_ref[s, :, head : 2 * head], across)
+            d_normed = d_normed + dot(block(1, s), w_ref[s, :, 2 * head : qkv], across)
+            pull = column(sections + s)
+            back = back + column(s) * (d_normed * g_ref[s]) - pull * acts[s].astype(F32)
             back = back.astype(BF16).astype(F32)
+    send_merged(0)
+    send_parts(3)
+    send_merged(1)
+
+    def finish(kind, out):
+        copies = messages(kind)
+        for number in (1, 2, 4, 5):
+            copies[number].wait_recv()
+        out[...] = (
+            part[kind, section].astype(F32)
+            + from_x[kind].astype(F32)
+            + from_y[kind].astype(F32)
+        )
+
+    finish(2, v_out)
+    send_merged(3)
+    finish(0, q_out)
+    finish(1, k_out)
+    finish(3, o_out)
+    for copy in sends:
+        copy.wait_send()
+
+
+def tail_call(x, c, made, scal, keep, w, g, collective_id):
+    reps, rows, shard = x.shape
+    sections = w.shape[0]
+    head = w.shape[2] // 4
+    total, half = reps * rows, shard // 2
+    chips = reps // 2
+    dma = pltpu.SemaphoreType.DMA
+    return pl.pallas_call(
+        tail_kernel,
+        out_shape=[jax.ShapeDtypeStruct((shard, head), F32)] * 4,
+        in_specs=vmem_specs(7),
+        out_specs=vmem_specs(4),
+        scratch_shapes=[
+            pltpu.VMEM((4, 2, chips) + made.shape[1:], BF16),
+            pltpu.VMEM((2, chips) + scal.shape, F32),
+            pltpu.VMEM((sections, total, shard), BF16),
+            pltpu.VMEM((sections, total, shard), BF16),
+            pltpu.VMEM((4, sections, shard, head), BF16),
+            pltpu.VMEM((4, 2, half, head), BF16),
+            pltpu.VMEM((4, shard, head), BF16),
+            pltpu.VMEM((4, shard, head), BF16),
+            pltpu.VMEM((4, 2, half, head), BF16),
+            dma((5, chips)), dma((5, chips)), dma((5, chips)), dma((5, chips)),
+            dma((4, 6)), dma((4, 6)),
+        ],
+        compiler_params=pltpu.CompilerParams(
+            collective_id=collective_id, has_side_effects=True, vmem_limit_bytes=VMEM_LIMIT
+        ),
+    )(x, c, made, scal, keep, w, g)
 
 
 def local_call(kernel, shapes, *arrays):
@@ -704,7 +798,7 @@
     made, scal = local_call(
         functools.partial(chain_kernel, head ** (-0.5)),
         [
-            jax.ShapeDtypeStruct((rows, sections * wide), BF16),
+            jax.ShapeDtypeStruct((4, rows, sections * head), BF16),
             jax.ShapeDtypeStruct((rows, head), F32),
         ],
         x_own,
@@ -712,21 +806,8 @@
         mixed,
         keep_own,
     )
-    made, scal = gather_call(made, scal, chips, 2)
-    (parts,) = local_call(
-        grads_kernel,
-        [jax.ShapeDtypeStruct((sections, shard, wide), BF16)],
-        x_shard,
-        c_shard,
-        made,
-        scal,
-        keep,
-        w_all,
-        g_all,
-    )
-    (parts,) = exchange([(parts, "section", True)], 3)
-    total = jnp.sum(parts.astype(F32), axis=0)
-    return tuple(total[None, :, i * head : (i + 1) * head] for i in range(4))
+    grads = tail_call(x_shard, c_shard, made, scal, keep, w_all, g_all, 2)
+    return tuple(grad[None] for grad in grads)
 
 
 def on_device(*arrays):

time: 138 us -> 126 us (0.913)
  Pallas kernels: 128 us -> 113 us
  local copies, waits for them, and re-layouts: 5.68 us -> 10.4 us
  other arithmetic: 3.35 us -> 1.34 us
    pallas_call x2 -> x1, Pallas kernels: 63.7 us -> 34.2 us  [exchange(): pl.pallas_call(functools.partial(exchange_kernel, tuple(plan), tuple(name...]
    pallas_call x1, Pallas kernels: 19.4 us -> 40.1 us  [tail_call(): pl.pallas_call(tail_kernel, out_shape=[jax.ShapeDtypeStruct((shard, head)...]
    pallas_call x3 -> x2, Pallas kernels: 17 us -> 10.7 us  [local_call(): pl.pallas_call(kernel, out_shape=shapes, in_specs=vmem_specs(len(arrays))...]
    unnamed x18 -> x24, local copies, waits for them, and re-layouts: 0.71 us -> 6.46 us
    reduce_sum x1 -> x0, other arithmetic: 2.01 us -> none  [low_rank(): total = jnp.sum(parts.astype(F32), axis=0)]
where the time goes in v3:
time: 126 us
  Pallas kernels  113 us (90%)
  local copies, waits for them, and re-layouts  10.4 us (8%)
  other arithmetic  1.34 us (1%)
    pallas_call x1, Pallas kernels, tail_call(): pl.pallas_call(tail_kernel, out_shape=[jax.ShapeDtypeStruct((shard, head)...  40.1 us
    pallas_call x1, Pallas kernels, exchange(): pl.pallas_call(functools.partial(exchange_kernel, tuple(plan), tuple(name...  34.2 us
    pallas_call x1, Pallas kernels, reduce_call(): pl.pallas_call(reduce_kernel, out_shape=[jax.ShapeDtypeStruct((chips,) +...  28 us
    pallas_call x2, Pallas kernels, local_call(): pl.pallas_call(kernel, out_shape=shapes, in_specs=vmem_specs(len(arrays))...  10.7 us
    unnamed x24, local copies, waits for them, and re-layouts  6.46 us

profile of v3, /device:TPU:0, one launch (start us, length us, event | category | flops | bytes accessed | tf_op | source)
XLA Modules:
  0.0 125.6 jit_solution(16292820610397289259)
XLA Ops:
  0.6 0.0 copy-start
  0.6 0.0 copy-start.7
  0.7 0.0 copy-start.6
  0.7 0.0 copy-start.5
  0.7 0.0 copy-start.4
  0.7 0.7 copy-done
  1.4 0.6 constant_dynamic-slice_fusion.2.refs_3_
  1.9 1.1 constant_dynamic-slice_fusion.3
  3.0 0.0 copy-start.1
  3.0 0.8 copy.23
  3.8 0.7 copy.22
  4.5 0.0 copy-done.7
  4.5 0.0 copy-done.6
  4.5 0.0 copy-done.5
  4.5 0.0 copy-done.4
  4.5 0.9 pad_maximum_fusion.refs_2_
  5.4 34.2 %shard_map.120 = (bf16[8,32,512]{2,1,0:T(8,128)(2,1)}, bf16[8,32,512]{2,1,0:T(8,128)(2,1)}, bf16[4,512,512]{2,1,0:T(8,128)(2,1)}, f32[4,1,512]{2,1,0:T(1,128)}) custom-call(bf16[8,32,512]{2,1,0:T(8,128)(2,1)} %bitcast.26, bf16[8,32,512]{2,1,0:T(8,128)(2,1)} %bitcast.27, bf16[512,512]{1,0:T(8,128)(2,1)} %pad_maximum_fusion.refs_2_, ...), custom_call_target="tpu_custom_call" | custom-call | tf_op jit(solution)/shard_map/pallas_call | solution.py:429
  39.6 0.0 copy-done.1
  39.6 4.5 %shard_map.121 = (bf16[2,4,32,2560]{3,2,1,0:T(8,128)(2,1)}, bf16[2,4,16,1280]{3,2,1,0:T(8,128)(2,1)}) custom-call(bf16[8,32,512]{2,1,0:T(8,128)(2,1)} %get-tuple-element.18.x_ref, bf16[8,32,512]{2,1,0:T(8,128)(2,1)} %get-tuple-element.19.c_ref, bf16[4,512,512]{2,1,0:T(8,128)(2,1)} %get-tuple-element.20.w_ref, f32[4,1,512]{2,1,0:T(1,128)} %get-tuple-element.21.g_ref), custom_call_target="tpu_custom_call" | custom-call | tf_op jit(solution)/shard_map/pallas_call | solution.py:732
  44.1 0.0 copy-start.9
  44.2 0.0 copy-start.8
  44.2 28.0 %shard_map.122 = (bf16[4,32,2560]{2,1,0:T(8,128)(2,1)}, bf16[2,4,4,16,1280]{4,3,2,1,0:T(8,128)(2,1)}) custom-call(bf16[2,4,32,2560]{3,2,1,0:T(8,128)(2,1)} %get-tuple-element.22.z_ref, bf16[2,4,16,1280]{3,2,1,0:T(8,128)(2,1)} %get-tuple-element.23.m_ref), custom_call_target="tpu_custom_call" | custom-call | tf_op jit(solution)/shard_map/pallas_call | solution.py:344
  72.2 0.0 copy-done.9
  72.2 0.1 constant_dynamic-slice_fusion.1
  72.3 0.1 and_select_fusion
  72.4 0.0 copy-done.8
  72.4 0.3 select_reduce_fusion
  72.7 0.1 fusion.1
  72.8 0.1 copy.17
  72.9 0.0 copy-start.2
  72.9 0.6 constant_dynamic-slice_fusion.keep_ref
  73.6 6.2 %shard_map.123 = (bf16[4,32,512]{2,1,0:T(8,128)(2,1)}, f32[32,128]{1,0:T(8,128)}) custom-call(bf16[32,4096]{1,0:T(8,128)(2,1)} %copy-done.1, bf16[4,32,2560]{2,1,0:T(8,128)(2,1)} %get-tuple-element.24.z_ref, bf16[2,4,4,16,1280]{4,3,2,1,0:T(8,128)(2,1)} %get-tuple-element.25.m_ref, f32[32,4]{1,0:T(8,128)} %constant_dynamic-slice_fusion.keep_ref), custom_call_target="tpu_custom_call" | custom-call | tf_op jit(solution)/shard_map/pallas_call | solution.py:732
  79.7 0.0 copy-done.2
  79.7 40.1 %shard_map.124 = (f32[512,128]{1,0:T(8,128)}, f32[512,128]{1,0:T(8,128)}, f32[512,128]{1,0:T(8,128)}, f32[512,128]{1,0:T(8,128)}) custom-call(bf16[8,32,512]{2,1,0:T(8,128)(2,1)} %get-tuple-element.18.x_ref, bf16[8,32,512]{2,1,0:T(8,128)(2,1)} %get-tuple-element.19.c_ref, bf16[4,32,512]{2,1,0:T(8,128)(2,1)} %get-tuple-element.26.made_ref, ...), custom_call_target="tpu_custom_call" | custom-call | tf_op jit(solution)/shard_map/pallas_call | solution.py:707
  119.8 0.0 copy-start.3
  119.8 1.7 %copy.28 = f32[1,512,128]{2,1,0:T(8,128)} copy(f32[1,512,128]{2,1,0:T(8,128)} %bitcast.34) | data formatting | bytes 524288
  121.5 1.7 %copy.29 = f32[1,512,128]{2,1,0:T(8,128)} copy(f32[1,512,128]{2,1,0:T(8,128)} %bitcast.33) | data formatting | bytes 524288
  123.2 1.7 %copy.30 = f32[1,512,128]{2,1,0:T(8,128)} copy(f32[1,512,128]{2,1,0:T(8,128)} %bitcast.32) | data formatting | bytes 524288
  124.9 0.0 copy-done.3
  124.9 0.7 copy.31
  (5 shorter events, 0.1 us)
Async XLA Ops:
  0.6 0.7 copy-start
  0.6 3.9 %copy-start.7 = (bf16[1,512,128]{2,1,0:T(8,128)(2,1)S(1)}, bf16[1,512,128]{2,1,0:T(8,128)(2,1)}, u32[]{:S(2)}) copy-start(bf16[1,512,128]{2,1,0:T(8,128)(2,1)} %param.11) | copy-start | bytes 393220
  0.7 3.9 %copy-start.6 = (bf16[1,512,128]{2,1,0:T(8,128)(2,1)S(1)}, bf16[1,512,128]{2,1,0:T(8,128)(2,1)}, u32[]{:S(2)}) copy-start(bf16[1,512,128]{2,1,0:T(8,128)(2,1)} %param.12) | copy-start | bytes 393220
  0.7 3.9 %copy-start.5 = (bf16[1,512,128]{2,1,0:T(8,128)(2,1)S(1)}, bf16[1,512,128]{2,1,0:T(8,128)(2,1)}, u32[]{:S(2)}) copy-start(bf16[1,512,128]{2,1,0:T(8,128)(2,1)} %param.13) | copy-start | bytes 393220
  0.7 3.9 %copy-start.4 = (bf16[1,512,128]{2,1,0:T(8,128)(2,1)S(1)}, bf16[1,512,128]{2,1,0:T(8,128)(2,1)}, u32[]{:S(2)}) copy-start(bf16[1,512,128]{2,1,0:T(8,128)(2,1)} %param.14) | copy-start | bytes 393220
  3.0 36.6 %copy-start.1 = (bf16[32,4096]{1,0:T(8,128)(2,1)}, bf16[32,4096]{1,0:T(8,128)(2,1)S(1)}, u32[]{:S(2)}) copy-start(bf16[32,4096]{1,0:T(8,128)(2,1)S(1)} %get-tuple-element.37.x_ref) | copy-start | bytes 786436
  44.1 28.0 %copy-start.9 = (s32[4,8]{1,0:T(4,128)S(1)}, s32[4,8]{1,0:T(4,128)}, u32[]{:S(2)}) copy-start(s32[4,8]{1,0:T(4,128)} %param.16) | copy-start | bytes 388
  44.2 28.3 %copy-start.8 = (s32[4,8]{1,0:T(4,128)S(1)}, s32[4,8]{1,0:T(4,128)}, u32[]{:S(2)}) copy-start(s32[4,8]{1,0:T(4,128)} %param.17) | copy-start | bytes 388
  72.9 6.8 %copy-start.2 = (f32[8,2,16,4]{3,2,1,0:T(8,128)}, f32[8,2,16,4]{3,2,1,0:T(8,128)S(1)}, u32[]{:S(2)}) copy-start(f32[8,2,16,4]{3,2,1,0:T(8,128)S(1)} %broadcast_in_dim.38) | copy-start | bytes 12292
  119.8 5.1 %copy-start.3 = (f32[512,128]{1,0:T(8,128)S(1)}, f32[512,128]{1,0:T(8,128)}, u32[]{:S(2)}) copy-start(f32[512,128]{1,0:T(8,128)} %get-tuple-element.31) | copy-start | bytes 786436

commit v4 on v3

--- a/solution.py
+++ b/solution.py
@@ -265,18 +265,128 @@
     return core, chip, section, partner, along, across
 
 
-def reduce_kernel(
-    z_ref, m_ref, z_land, m_out, z_core, m_core, z_sum, m_sum, m_land, m_total,
+def dot(left, right, dims=((1,), (0,))):
+    return lax.dot_general(left, right, (dims, ((), ())), preferred_element_type=F32)
+
+
+def front_kernel(
+    x_in, c_in, w_in, g_in,
+    x_ref, c_ref, w_ref, g_ref, z_land, m_out,
+    z_ref, z_core, z_sum, m_ref, m_core, m_sum, m_land, m_total,
     core_send, core_recv, z_send, z_recv, m_send, m_recv, g_send, g_recv, s_send, s_recv,
+    x_send, x_recv, w_send, w_recv,
 ):
-    chips, sections = z_land.shape[0], m_out.shape[1]
+    sections, chips = z_land.shape[:2]
+    reps, rows, shard = x_ref.shape
+    head = w_ref.shape[2] // 4
+    qkv = 3 * head
+    half = shard // 2
     core, chip, section, partner, along, across = place(chips, sections)
-    greet([partner] + [a[3] for a in along] + [a[3] for a in across])
     other = 1 - core
+    near_x = section + 1 - 2 * lax.rem(section, 2)
+    near_y = lax.rem(section + 2, 4)
+    diagonal = 3 - section
+    to_x, to_y = {"section": near_x}, {"section": near_y}
+    me = chip * 2 + core
+    peers = []
+    for step in range(1, reps):
+        to, source = lax.rem(me + step, reps), lax.rem(me + reps - step, reps)
+        peers.append((step, to, slot("rep", source, reps), {"rep": to}))
+    greet([p[3] for p in peers] + [a[3] for a in across])
+    sends = []
+
+    def start(copy):
+        copy.start()
+        sends.append(copy)
+
+    first, second = pl.ds(0, half), pl.ds(half, half)
+
+    def weight(number, src, at, rows_at, target):
+        dst = w_ref.at[at, rows_at]
+        return remote(src, dst, w_send.at[number], w_recv.at[number], target)
+
+    start(weight(0, w_in.at[first], section, first, to_x))
+    start(weight(1, w_in.at[second], section, second, to_y))
+    for step, to, source, target in across:
+        start(remote(g_in, g_ref.at[section], w_send.at[5 + step], w_recv.at[5 + step], target))
+    start(weight(2, w_in.at[second], section, second, to_x))
+    start(weight(3, w_in.at[first], section, first, to_y))
+    mine = slot("rep", me, reps)
+    for i, (src, dst) in enumerate(((x_in, x_ref), (c_in, c_ref))):
+        for step, to, source, target in peers:
+            start(remote(src.at[to], dst.at[mine], x_send.at[i, step], x_recv.at[i, step], target))
+        dst[mine] = src[me]
+    w_ref[section] = w_in[...]
+    g_ref[section] = g_in[...]
+
+    def landed(number, at, rows_at):
+        ref = w_ref.at[at, rows_at]
+        remote(ref, ref, w_send.at[number], w_recv.at[number], to_x).wait_recv()
+
+    landed(0, near_x, first)
+    start(weight(4, w_ref.at[near_x, first], near_x, first, to_y))
+    landed(1, near_y, second)
+    start(weight(5, w_ref.at[near_y, second], near_y, second, to_x))
+    for step, to, source, target in across:
+        at = g_ref.at[source]
+        remote(at, at, w_send.at[5 + step], w_recv.at[5 + step], target).wait_recv()
+    for i, dst in enumerate((x_ref, c_ref)):
+        for step, to, source, target in peers:
+            at = dst.at[source]
+            remote(at, at, x_send.at[i, step], x_recv.at[i, step], target).wait_recv()
+    x_all = x_ref[...].reshape(reps * rows, shard)
+    c_all = c_ref[...].reshape(reps * rows, shard)
+    wide = x_all.astype(F32)
+
+    def put(ref, at, block):
+        shape = ref.shape[:3] + (block.shape[1],)
+        ref[:, :, :, at : at + block.shape[1]] = block.astype(BF16).reshape(shape)
+
+    def chunk(i, s):
+        scaled = (wide * g_ref[s]).astype(BF16)
+        w_o = w_ref[s, :, qkv:]
+        z = z_ref.at[i]
+        put(z, 0, dot(scaled, w_ref[s, :, 0:qkv]))
+        put(z, qkv, dot(x_all, w_o))
+        put(z, 4 * head, dot(c_all, w_o))
+        copy = remote(
+            z_ref.at[i, other], z_core.at[i], core_send.at[8 + i], core_recv.at[8 + i], partner
+        )
+        copy.start()
+        return copy
+
+    z_copies = []
+
+    def forward(i, s, copy):
+        copy.wait()
+        z_sum[i] = (z_ref[i, core].astype(F32) + z_core[i].astype(F32)).astype(BF16)
+        for step, to, source, target in along:
+            copy = remote(
+                z_sum.at[i, to], z_land.at[s, step], z_send.at[i, step], z_recv.at[i, step], target
+            )
+            copy.start()
+            z_copies.append(copy)
+        z_land[s, 0] = z_sum[i, chip]
+
+    forward(0, section, chunk(0, section))
+    landed(2, near_x, second)
+    forward(1, near_x, chunk(1, near_x))
+    landed(3, near_y, first)
+    landed(4, diagonal, first)
+    landed(5, diagonal, second)
+    for gap in range(1, sections // 2 + 1):
+        far = lax.rem(section + gap, sections)
+        low, high = jnp.minimum(section, far), jnp.maximum(section, far)
+        turned = jnp.transpose(w_ref[low, :, qkv:].astype(F32))
+        turned = (turned * g_ref[high]).astype(BF16)
+        put(m_ref, (gap - 1) * qkv, dot(turned, w_ref[high, :, 0:qkv]))
+    w_me = w_ref[section, :, qkv:]
+    base = sections // 2 * qkv
+    for s in range(sections):
+        put(m_ref, base + s * head, dot(w_me, w_ref[s, :, qkv:], ((0,), (0,))))
     m_first = remote(m_ref.at[other], m_core, core_send.at[0], core_recv.at[0], partner)
     m_first.start()
-    z_first = remote(z_ref.at[other], z_core, core_send.at[1], core_recv.at[1], partner)
-    z_first.start()
+    chunk_y = chunk(2, near_y)
     m_first.wait()
     m_sum[...] = (m_ref[core].astype(F32) + m_core[...].astype(F32)).astype(BF16)
     m_copies = []
@@ -285,8 +395,7 @@
         copy.start()
         m_copies.append(copy)
     total = m_sum[chip].astype(F32)
-    z_first.wait()
-    z_sum[...] = (z_ref[core].astype(F32) + z_core[...].astype(F32)).astype(BF16)
+    chunk_d = chunk(3, diagonal)
     for copy, (step, to, source, target) in zip(m_copies, along):
         copy.wait()
         total = total + m_land[step].astype(F32)
@@ -298,13 +407,9 @@
         )
         copy.start()
         spread.append(copy)
-    z_copies = []
-    for step, to, source, target in along:
-        copy = remote(z_sum.at[to], z_land.at[step], z_send.at[step], z_recv.at[step], target)
-        copy.start()
-        z_copies.append(copy)
     m_out[core, section, chip] = total.astype(BF16)
-    z_land[0] = z_sum[chip]
+    forward(2, near_y, chunk_y)
+    forward(3, diagonal, chunk_d)
     for copy, (step, to, source, target) in zip(spread, along):
         copy.wait_send()
         at = m_out.at[core, section, source]
@@ -335,142 +440,48 @@
         copy.wait_send()
         at = m_out.at[other, source]
         remote(at, at, core_send.at[2 + step], core_recv.at[2 + step], partner).wait_recv()
-
-
-def reduce_call(z, m, sections, collective_id):
-    two, chips = z.shape[:2]
-    block, mix = z.shape[2:], m.shape[2:]
+    for copy in sends:
+        copy.wait_send()
+
+
+def front_call(x, c, w, g, collective_id):
+    reps, rows, shard = x.shape
+    head = w.shape[1] // 4
+    sections = lax.axis_size("section")
+    chips = reps // 2
+    block = (rows, 5 * head)
+    mix = (head // reps, sections // 2 * 3 * head + sections * head)
     dma = pltpu.SemaphoreType.DMA
     return pl.pallas_call(
-        reduce_kernel,
+        front_kernel,
         out_shape=[
-            jax.ShapeDtypeStruct((chips,) + block, BF16),
-            jax.ShapeDtypeStruct((two, sections, chips) + mix, BF16),
+            jax.ShapeDtypeStruct(x.shape, BF16),
+            jax.ShapeDtypeStruct(x.shape, BF16),
+            jax.ShapeDtypeStruct((sections,) + w.shape, BF16),
+            jax.ShapeDtypeStruct((sections,) + g.shape, F32),
+            jax.ShapeDtypeStruct((sections, chips) + block, BF16),
+            jax.ShapeDtypeStruct((2, sections, chips) + mix, BF16),
         ],
-        in_specs=vmem_specs(2),
-        out_specs=vmem_specs(2),
+        in_specs=vmem_specs(4),
+        out_specs=vmem_specs(6),
         scratch_shapes=[
-            pltpu.VMEM((chips,) + block, BF16),
+            pltpu.VMEM((sections, 2, chips) + block, BF16),
+            pltpu.VMEM((sections, chips) + block, BF16),
+            pltpu.VMEM((sections, chips) + block, BF16),
+            pltpu.VMEM((2, chips) + mix, BF16),
             pltpu.VMEM((chips,) + mix, BF16),
-            pltpu.VMEM((chips,) + block, BF16),
             pltpu.VMEM((chips,) + mix, BF16),
             pltpu.VMEM((chips,) + mix, BF16),
             pltpu.VMEM(mix, BF16),
-            dma((2 + sections,)), dma((2 + sections,)),
-            dma((chips,)), dma((chips,)), dma((chips,)), dma((chips,)),
+            dma((12,)), dma((12,)),
+            dma((sections, chips)), dma((sections, chips)), dma((chips,)), dma((chips,)),
             dma((chips,)), dma((chips,)), dma((sections,)), dma((sections,)),
+            dma((2, reps)), dma((2, reps)), dma((9,)), dma((9,)),
         ],
         compiler_params=pltpu.CompilerParams(
             collective_id=collective_id, has_side_effects=True, vmem_limit_bytes=VMEM_LIMIT
         ),
-    )(z, m)
-
-
-def exchange_kernel(plan, axes, *refs):
-    count = len(plan)
-    ins, outs = refs[:count], refs[count : 2 * count]
-    sems = refs[2 * count :]
-    barrier = pltpu.get_barrier_semaphore()
-    waits = 0
-    for axis, size in axes:
-        me = lax.axis_index(axis)
-        for step in range(1, size):
-            peer = lax.rem(me + step, size)
-            pl.semaphore_signal(
-                barrier, inc=1, device_id={axis: peer}, device_id_type=pl.DeviceIdType.MESH
-            )
-            waits += 1
-    pl.semaphore_wait(barrier, waits)
-    copies = []
-    for i, (axis, size, split) in enumerate(plan):
-        send, recv = sems[2 * i], sems[2 * i + 1]
-        me = lax.axis_index(axis)
-        for step in range(1, size):
-            peer = lax.rem(me + step, size)
-            copy = pltpu.make_async_remote_copy(
-                src_ref=ins[i].at[peer] if split else ins[i],
-                dst_ref=outs[i].at[slot(axis, me, size)],
-                send_sem=send.at[step],
-                recv_sem=recv.at[step],
-                device_id={axis: peer},
-                device_id_type=pl.DeviceIdType.MESH,
-            )
-            copy.start()
-            copies.append((i, axis, size, split, step, copy))
-    for i, (axis, size, split) in enumerate(plan):
-        me = lax.axis_index(axis)
-        own = ins[i].at[me] if split else ins[i]
-        outs[i][slot(axis, me, size)] = own[...]
-    for i, axis, size, split, step, copy in copies:
-        copy.wait_send()
-        me = lax.axis_index(axis)
-        source = lax.rem(me + size - step, size)
-        at = slot(axis, source, size)
-        pltpu.make_async_remote_copy(
-            src_ref=outs[i].at[at],
-            dst_ref=outs[i].at[at],
-            send_sem=sems[2 * i].at[step],
-            recv_sem=sems[2 * i + 1].at[step],
-            device_id={axis: source},
-            device_id_type=pl.DeviceIdType.MESH,
-        ).wait_recv()
-
-
-def exchange(items, collective_id):
-    plan, shapes, scratch, names = [], [], [], []
-    for array, axis, split in items:
-        size = lax.axis_size(axis)
-        plan.append((axis, size, split))
-        block = array.shape[1:] if split else array.shape
-        shapes.append(jax.ShapeDtypeStruct((size,) + block, array.dtype))
-        scratch += [pltpu.SemaphoreType.DMA((size,)), pltpu.SemaphoreType.DMA((size,))]
-        if (axis, size) not in names:
-            names.append((axis, size))
-    return pl.pallas_call(
-        functools.partial(exchange_kernel, tuple(plan), tuple(names)),
-        out_shape=shapes,
-        in_specs=vmem_specs(len(items)),
-        out_specs=vmem_specs(len(items)),
-        scratch_shapes=scratch,
-        compiler_params=pltpu.CompilerParams(
-            collective_id=collective_id, has_side_effects=True, vmem_limit_bytes=VMEM_LIMIT
-        ),
-    )(*[array for array, _, _ in items])
-
-
-def dot(left, right, dims=((1,), (0,))):
-    return lax.dot_general(left, right, (dims, ((), ())), preferred_element_type=F32)
-
-
-def project_kernel(x_ref, c_ref, w_ref, g_ref, z_ref, m_ref):
-    reps, rows, shard = x_ref.shape
-    sections = w_ref.shape[0]
-    head = w_ref.shape[2] // 4
-    qkv = 3 * head
-    me = lax.axis_index("section")
-    x_all = x_ref[...].reshape(reps * rows, shard)
-    c_all = c_ref[...].reshape(reps * rows, shard)
-    wide = x_all.astype(F32)
-
-    def put(ref, at, block):
-        shape = ref.shape[:3] + (block.shape[1],)
-        ref[:, :, :, at : at + block.shape[1]] = block.astype(BF16).reshape(shape)
-
-    for gap in range(1, sections // 2 + 1):
-        far = lax.rem(me + gap, sections)
-        low, high = jnp.minimum(me, far), jnp.maximum(me, far)
-        turned = jnp.transpose(w_ref[low, :, qkv:].astype(F32))
-        turned = (turned * g_ref[high]).astype(BF16)
-        put(m_ref, (gap - 1) * qkv, dot(turned, w_ref[high, :, 0:qkv]))
-    w_me = w_ref[me, :, qkv:]
-    base = sections // 2 * qkv
-    for s in range(sections):
-        scaled = (wide * g_ref[s]).astype(BF16)
-        w_o = w_ref[s, :, qkv:]
-        put(z_ref, s * 4 * head, dot(scaled, w_ref[s, :, 0:qkv]))
-        put(z_ref, s * 4 * head + qkv, dot(x_all, w_o))
-        put(z_ref, (sections * 4 + s) * head, dot(c_all, w_o))
-        put(m_ref, base + s * head, dot(w_me, w_o, ((0,), (0,))))
+    )(x, c, w, g)
 
 
 def chain_kernel(scale, x_ref, z_ref, m_ref, keep_ref, out_ref, scal_ref):
@@ -480,8 +491,7 @@
     wide = 4 * head
     x_float = x_ref[...].astype(F32)
     square = jnp.sum(x_float * x_float, axis=1, keepdims=True)
-    z = jnp.sum(z_ref[...].astype(F32), axis=0)
-    back = z[:, sections * wide :]
+    z = [jnp.sum(z_ref[s].astype(F32), axis=0) for s in range(sections)]
     base = sections // 2 * 3 * head
     mix = [
         jnp.concatenate([m_ref[c, s].reshape(head // 2, -1) for c in range(2)], axis=0)
@@ -498,8 +508,8 @@
     row = lax.broadcasted_iota(jnp.int32, (rows, rows), 0)
     col = lax.broadcasted_iota(jnp.int32, (rows, rows), 1)
     allowed = (row >= col) & (row // ROWS == col // ROWS)
-    y = [z[:, s * wide : s * wide + 3 * head] for s in range(sections)]
-    acto = [z[:, s * wide + 3 * head : (s + 1) * wide] for s in range(sections)]
+    y = [z[s][:, 0 : 3 * head] for s in range(sections)]
+    acto = [z[s][:, 3 * head : wide] for s in range(sections)]
     saved = []
     for s in range(sections):
         keep = keep_ref[:, s : s + 1]
@@ -525,7 +535,7 @@
             if t > s:
                 y[t] = y[t] + dot(kept_low, pair(s, t))
             acto[t] = acto[t] + moved[:, t * head : (t + 1) * head]
-    bo = [back[:, s * head : (s + 1) * head] for s in range(sections)]
+    bo = [z[s][:, wide:] for s in range(sections)]
     lane = lax.broadcasted_iota(jnp.int32, (rows, head), 1)
     scal = jnp.zeros((rows, head), F32)
     for s in range(sections - 1, -1, -1):
@@ -555,7 +565,7 @@
 
 def tail_kernel(
     x_ref, c_ref, made_ref, scal_ref, keep_ref, w_ref, g_ref,
-    q_out, k_out, v_out, o_out,
+    out_ref,
     made, scal, normed, acts, part, relay, from_x, from_y, merged,
     z_send, z_recv, core_send, core_recv, h_send, h_recv,
 ):
@@ -678,21 +688,21 @@
     send_parts(3)
     send_merged(1)
 
-    def finish(kind, out):
+    def finish(kind):
         copies = messages(kind)
         for number in (1, 2, 4, 5):
             copies[number].wait_recv()
-        out[...] = (
+        out_ref[kind] = (
             part[kind, section].astype(F32)
             + from_x[kind].astype(F32)
             + from_y[kind].astype(F32)
         )
 
-    finish(2, v_out)
+    finish(2)
     send_merged(3)
-    finish(0, q_out)
-    finish(1, k_out)
-    finish(3, o_out)
+    finish(0)
+    finish(1)
+    finish(3)
     for copy in sends:
         copy.wait_send()
 
@@ -706,9 +716,9 @@
     dma = pltpu.SemaphoreType.DMA
     return pl.pallas_call(
         tail_kernel,
-        out_shape=[jax.ShapeDtypeStruct((shard, head), F32)] * 4,
+        out_shape=[jax.ShapeDtypeStruct((4, shard, head), F32)],
         in_specs=vmem_specs(7),
-        out_specs=vmem_specs(4),
+        out_specs=vmem_specs(1),
         scratch_shapes=[
             pltpu.VMEM((4, 2, chips) + made.shape[1:], BF16),
             pltpu.VMEM((2, chips) + scal.shape, F32),
@@ -773,28 +783,7 @@
     keep = jnp.broadcast_to(keep[:, :, None, :], (reps, batches, ROWS, sections))
     keep = keep.reshape(reps * rows, sections)
     keep_own = lax.dynamic_slice_in_dim(keep, slot("rep", rep_pos, reps) * rows, rows, 0)
-    x_shard, c_shard, w_all, g_all = exchange(
-        [
-            (x_split, "rep", True),
-            (c_split, "rep", True),
-            (w_pack, "section", False),
-            (g_own, "section", False),
-        ],
-        0,
-    )
-    mix_width = sections // 2 * 3 * head + sections * head
-    z, mixed = local_call(
-        project_kernel,
-        [
-            jax.ShapeDtypeStruct((2, chips, rows, sections * 5 * head), BF16),
-            jax.ShapeDtypeStruct((2, chips, head // reps, mix_width), BF16),
-        ],
-        x_shard,
-        c_shard,
-        w_all,
-        g_all,
-    )
-    z, mixed = reduce_call(z, mixed, sections, 1)
+    x_shard, c_shard, w_all, g_all, z, mixed = front_call(x_split, c_split, w_pack, g_own, 0)
     made, scal = local_call(
         functools.partial(chain_kernel, head ** (-0.5)),
         [
@@ -806,8 +795,8 @@
         mixed,
         keep_own,
     )
-    grads = tail_call(x_shard, c_shard, made, scal, keep, w_all, g_all, 2)
-    return tuple(grad[None] for grad in grads)
+    (grads,) = tail_call(x_shard, c_shard, made, scal, keep, w_all, g_all, 2)
+    return tuple(grads[i][None] for i in range(4))
 
 
 def on_device(*arrays):

time: 126 us -> 104 us (0.83)
  Pallas kernels: 113 us -> 95.4 us
  local copies, waits for them, and re-layouts: 10.4 us -> 6.28 us
    pallas_call x3 -> x2, Pallas kernels: 102 us -> 89.3 us  [the longest x1 49.9 us: front_call(): pl.pallas_call(front_kernel, out_shape=[jax.ShapeDtypeStruct(x.shape, BF1...]
    unnamed x24 -> x18, local copies, waits for them, and re-layouts: 6.46 us -> 0.05 us
    pallas_call x2 -> x1, Pallas kernels: 10.7 us -> 6.16 us  [local_call(): pl.pallas_call(kernel, out_shape=shapes, in_specs=vmem_specs(len(arrays))...]
    slice x0 -> x1, local copies, waits for them, and re-layouts: none -> 2.17 us  [low_rank(): return tuple((grads[i][None] for i in range(4)))]
where the time goes in v4:
time: 104 us
  Pallas kernels  95.4 us (92%)
  local copies, waits for them, and re-layouts  6.28 us (6%)
  other arithmetic  1.35 us (1%)
    pallas_call x1, Pallas kernels, front_call(): pl.pallas_call(front_kernel, out_shape=[jax.ShapeDtypeStruct(x.shape, BF1...  49.9 us
    pallas_call x1, Pallas kernels, tail_call(): pl.pallas_call(tail_kernel, out_shape=[jax.ShapeDtypeStruct((4, shard, he...  39.4 us
    pallas_call x1, Pallas kernels, local_call(): pl.pallas_call(kernel, out_shape=shapes, in_specs=vmem_specs(len(arrays))...  6.16 us
    slice x1, local copies, waits for them, and re-layouts, low_rank(): return tuple((grads[i][None] for i in range(4)))  2.17 us

profile of v4, /device:TPU:0, one launch (start us, length us, event | category | flops | bytes accessed | tf_op | source)
XLA Modules:
  0.0 103.9 jit_solution(3717628805040453438)
XLA Ops:
  0.6 0.0 copy-start
  0.6 0.0 copy-start.3
  0.7 0.0 copy-start.4
  0.7 0.0 copy-start.5
  0.7 0.0 copy-start.6
  0.7 0.0 copy-start.8
  0.7 0.0 copy-start.7
  0.7 1.2 %constant_dynamic-slice_fusion.3 = (bf16[32,4096]{1,0:T(8,128)(2,1)S(1)}, bf16[32,4096]{1,0:T(8,128)(2,1)S(1)}) fusion(bf16[128,4096]{1,0:T(8,128)(2,1)} %param.10, s32[]{:T(128)S(6)} %select_n.71, bf16[128,4096]{1,0:T(8,128)(2,1)} %param.9), kind=kLoop, calls=%fused_computation.30 | loop fusion | bytes 1048580 | tf_op jit(solution)/shard_map/dynamic_slice | solution.py:763
  1.9 0.0 copy-start.1
  1.9 0.8 copy.23
  2.7 0.7 copy.22
  3.4 0.0 copy-done.3
  3.4 0.0 copy-done.4
  3.4 0.0 copy-done.5
  3.4 0.0 copy-done.6
  3.4 0.9 pad_maximum_fusion.w_in
  4.3 0.0 copy-done
  4.3 0.6 constant_dynamic-slice_fusion.2.g_in
  4.9 49.9 %shard_map.120 = (bf16[8,32,512]{2,1,0:T(8,128)(2,1)}, bf16[8,32,512]{2,1,0:T(8,128)(2,1)}, bf16[4,512,512]{2,1,0:T(8,128)(2,1)}, f32[4,1,512]{2,1,0:T(1,128)}, ...) custom-call(bf16[8,32,512]{2,1,0:T(8,128)(2,1)} %bitcast.22, bf16[8,32,512]{2,1,0:T(8,128)(2,1)} %bitcast.23, ...), custom_call_target="tpu_custom_call" | custom-call | tf_op jit(solution)/shard_map/pallas_call | solution.py:455
  54.7 0.0 copy-done.8
  54.8 0.1 constant_dynamic-slice_fusion.1
  54.9 0.1 and_select_fusion
  54.9 0.0 copy-done.7
  55.0 0.3 select_reduce_fusion
  55.3 0.1 fusion.1
  55.3 0.1 copy.17
  55.4 0.0 copy-start.2
  55.5 0.6 constant_dynamic-slice_fusion.keep_ref
  56.1 0.0 copy-done.1
  56.1 6.2 %shard_map.121 = (bf16[4,32,512]{2,1,0:T(8,128)(2,1)}, f32[32,128]{1,0:T(8,128)}) custom-call(bf16[32,4096]{1,0:T(8,128)(2,1)} %copy-done.1, bf16[4,4,32,640]{3,2,1,0:T(8,128)(2,1)} %get-tuple-element.14.z_ref, bf16[2,4,4,16,1280]{4,3,2,1,0:T(8,128)(2,1)} %get-tuple-element.15.m_ref, f32[32,4]{1,0:T(8,128)} %constant_dynamic-slice_fusion.keep_ref), custom_call_target="tpu_custom_call" | custom-call | tf_op jit(solution)/shard_map/pallas_call | solution.py:742
  62.3 0.0 copy-done.2
  62.3 39.4 %shard_map.122 = f32[4,512,128]{2,1,0:T(8,128)} custom-call(bf16[8,32,512]{2,1,0:T(8,128)(2,1)} %get-tuple-element.12.x_ref, bf16[8,32,512]{2,1,0:T(8,128)(2,1)} %get-tuple-element.13.c_ref, bf16[4,32,512]{2,1,0:T(8,128)(2,1)} %get-tuple-element.16.made_ref, f32[32,128]{1,0:T(8,128)} %get-tuple-element.17.scal_ref, f32[256,4]{1,0:T(8,128)} %bitcast.26, ...), custom_call_target="tpu_custom_call" | custom-call | tf_op jit(solution)/shard_map/pallas_call | solution.py:717
  101.7 2.2 %fusion.8 = (f32[1,512,128]{2,1,0:T(8,128)}, f32[1,512,128]{2,1,0:T(8,128)}, f32[1,512,128]{2,1,0:T(8,128)}, f32[1,512,128]{2,1,0:T(8,128)}) fusion(f32[4,512,128]{2,1,0:T(8,128)} %shard_map.122), kind=kLoop, calls=%fused_computation.44 | loop fusion | bytes 2097152 | tf_op jit(solution)/shard_map/slice | solution.py:799
  (5 shorter events, 0.1 us)
Async XLA Ops:
  0.6 3.7 %copy-start = (f32[1,4096]{1,0:T(1,128)S(1)}, f32[1,4096]{1,0:T(1,128)}, u32[]{:S(2)}) copy-start(f32[1,4096]{1,0:T(1,128)} %param.15) | copy-start | bytes 49156
  0.6 2.8 %copy-start.3 = (bf16[1,512,128]{2,1,0:T(8,128)(2,1)S(1)}, bf16[1,512,128]{2,1,0:T(8,128)(2,1)}, u32[]{:S(2)}) copy-start(bf16[1,512,128]{2,1,0:T(8,128)(2,1)} %param.14) | copy-start | bytes 393220
  0.7 2.8 %copy-start.4 = (bf16[1,512,128]{2,1,0:T(8,128)(2,1)S(1)}, bf16[1,512,128]{2,1,0:T(8,128)(2,1)}, u32[]{:S(2)}) copy-start(bf16[1,512,128]{2,1,0:T(8,128)(2,1)} %param.13) | copy-start | bytes 393220
  0.7 2.7 %copy-start.5 = (bf16[1,512,128]{2,1,0:T(8,128)(2,1)S(1)}, bf16[1,512,128]{2,1,0:T(8,128)(2,1)}, u32[]{:S(2)}) copy-start(bf16[1,512,128]{2,1,0:T(8,128)(2,1)} %param.12) | copy-start | bytes 393220
  0.7 2.7 %copy-start.6 = (bf16[1,512,128]{2,1,0:T(8,128)(2,1)S(1)}, bf16[1,512,128]{2,1,0:T(8,128)(2,1)}, u32[]{:S(2)}) copy-start(bf16[1,512,128]{2,1,0:T(8,128)(2,1)} %param.11) | copy-start | bytes 393220
  0.7 54.0 %copy-start.8 = (s32[4,8]{1,0:T(4,128)S(1)}, s32[4,8]{1,0:T(4,128)}, u32[]{:S(2)}) copy-start(s32[4,8]{1,0:T(4,128)} %param.16) | copy-start | bytes 388
  0.7 54.2 %copy-start.7 = (s32[4,8]{1,0:T(4,128)S(1)}, s32[4,8]{1,0:T(4,128)}, u32[]{:S(2)}) copy-start(s32[4,8]{1,0:T(4,128)} %param.17) | copy-start | bytes 388
  1.9 54.2 %copy-start.1 = (bf16[32,4096]{1,0:T(8,128)(2,1)}, bf16[32,4096]{1,0:T(8,128)(2,1)S(1)}, u32[]{:S(2)}) copy-start(bf16[32,4096]{1,0:T(8,128)(2,1)S(1)} %get-tuple-element.29.x_ref) | copy-start | bytes 786436
  55.4 6.8 %copy-start.2 = (f32[8,2,16,4]{3,2,1,0:T(8,128)}, f32[8,2,16,4]{3,2,1,0:T(8,128)S(1)}, u32[]{:S(2)}) copy-start(f32[8,2,16,4]{3,2,1,0:T(8,128)S(1)} %broadcast_in_dim.16) | copy-start | bytes 12292

commit v5 on v4

--- a/solution.py
+++ b/solution.py
@@ -272,12 +272,13 @@
 def front_kernel(
     x_in, c_in, w_in, g_in,
     x_ref, c_ref, w_ref, g_ref, z_land, m_out,
-    z_ref, z_core, z_sum, m_ref, m_core, m_sum, m_land, m_total,
+    z_ref, z_core, z_sum, z_mid, z_far, m_ref, m_core, m_sum, m_land, m_total,
     core_send, core_recv, z_send, z_recv, m_send, m_recv, g_send, g_recv, s_send, s_recv,
     x_send, x_recv, w_send, w_recv,
 ):
-    sections, chips = z_land.shape[:2]
+    sections = z_land.shape[0]
     reps, rows, shard = x_ref.shape
+    chips = reps // 2
     head = w_ref.shape[2] // 4
     qkv = 3 * head
     half = shard // 2
@@ -312,10 +313,12 @@
     start(weight(2, w_in.at[second], section, second, to_x))
     start(weight(3, w_in.at[first], section, first, to_y))
     mine = slot("rep", me, reps)
+    own_rows = pl.ds(pl.multiple_of(section * rows, rows), rows)
     for i, (src, dst) in enumerate(((x_in, x_ref), (c_in, c_ref))):
         for step, to, source, target in peers:
-            start(remote(src.at[to], dst.at[mine], x_send.at[i, step], x_recv.at[i, step], target))
-        dst[mine] = src[me]
+            at = src.at[own_rows, pl.ds(pl.multiple_of(to * shard, shard), shard)]
+            start(remote(at, dst.at[mine], x_send.at[i, step], x_recv.at[i, step], target))
+        dst[mine] = src[own_rows, pl.ds(pl.multiple_of(me * shard, shard), shard)]
     w_ref[section] = w_in[...]
     g_ref[section] = g_in[...]
 
@@ -355,22 +358,36 @@
         copy.start()
         return copy
 
-    z_copies = []
+    z_copies, halves = [], []
+    beside = chip + 1 - 2 * lax.rem(chip, 2)
+    away = lax.rem(chip + 2, 4)
+    to_beside, to_away = {"rep": beside * 2 + core}, {"rep": away * 2 + core}
 
     def forward(i, s, copy):
         copy.wait()
         z_sum[i] = (z_ref[i, core].astype(F32) + z_core[i].astype(F32)).astype(BF16)
-        for step, to, source, target in along:
+        for j, to in ((1, lax.rem(beside + 2, 4)), (0, beside)):
             copy = remote(
-                z_sum.at[i, to], z_land.at[s, step], z_send.at[i, step], z_recv.at[i, step], target
+                z_sum.at[i, to], z_mid.at[i, j], z_send.at[i, j], z_recv.at[i, j], to_beside
             )
             copy.start()
-            z_copies.append(copy)
-        z_land[s, 0] = z_sum[i, chip]
+            halves.append((i, j, copy))
+
+    def second_hop(i, s):
+        for at, j, copy in halves:
+            if at == i:
+                copy.wait()
+        z_far[i] = (z_sum[i, away].astype(F32) + z_mid[i, 1].astype(F32)).astype(BF16)
+        copy = remote(z_far.at[i], z_land.at[s, 1], z_send.at[i, 2], z_recv.at[i, 2], to_away)
+        copy.start()
+        z_copies.append(copy)
+        z_land[s, 0] = (z_sum[i, chip].astype(F32) + z_mid[i, 0].astype(F32)).astype(BF16)
 
     forward(0, section, chunk(0, section))
     landed(2, near_x, second)
-    forward(1, near_x, chunk(1, near_x))
+    chunk_x = chunk(1, near_x)
+    second_hop(0, section)
+    forward(1, near_x, chunk_x)
     landed(3, near_y, first)
     landed(4, diagonal, first)
     landed(5, diagonal, second)
@@ -396,6 +413,7 @@
         m_copies.append(copy)
     total = m_sum[chip].astype(F32)
     chunk_d = chunk(3, diagonal)
+    second_hop(1, near_x)
     for copy, (step, to, source, target) in zip(m_copies, along):
         copy.wait()
         total = total + m_land[step].astype(F32)
@@ -422,6 +440,8 @@
         cross.append(copy)
     own = remote(mine, mine, core_send.at[2], core_recv.at[2], partner)
     own.start()
+    second_hop(2, near_y)
+    second_hop(3, diagonal)
     last = []
     for copy, (step, to, source, target) in zip(cross, across):
         at = m_out.at[core, source]
@@ -444,8 +464,9 @@
         copy.wait_send()
 
 
-def front_call(x, c, w, g, collective_id):
-    reps, rows, shard = x.shape
+def front_call(x, c, w, g, rows, collective_id):
+    shard = w.shape[0]
+    reps = x.shape[1] // shard
     head = w.shape[1] // 4
     sections = lax.axis_size("section")
     chips = reps // 2
@@ -455,11 +476,11 @@
     return pl.pallas_call(
         front_kernel,
         out_shape=[
-            jax.ShapeDtypeStruct(x.shape, BF16),
-            jax.ShapeDtypeStruct(x.shape, BF16),
+            jax.ShapeDtypeStruct((reps, rows, shard), BF16),
+            jax.ShapeDtypeStruct((reps, rows, shard), BF16),
             jax.ShapeDtypeStruct((sections,) + w.shape, BF16),
             jax.ShapeDtypeStruct((sections,) + g.shape, F32),
-            jax.ShapeDtypeStruct((sections, chips) + block, BF16),
+            jax.ShapeDtypeStruct((sections, 2) + block, BF16),
             jax.ShapeDtypeStruct((2, sections, chips) + mix, BF16),
         ],
         in_specs=vmem_specs(4),
@@ -468,6 +489,8 @@
             pltpu.VMEM((sections, 2, chips) + block, BF16),
             pltpu.VMEM((sections, chips) + block, BF16),
             pltpu.VMEM((sections, chips) + block, BF16),
+            pltpu.VMEM((sections, 2) + block, BF16),
+            pltpu.VMEM((sections,) + block, BF16),
             pltpu.VMEM((2, chips) + mix, BF16),
             pltpu.VMEM((chips,) + mix, BF16),
             pltpu.VMEM((chips,) + mix, BF16),
@@ -487,9 +510,10 @@
 def chain_kernel(scale, x_ref, z_ref, m_ref, keep_ref, out_ref, scal_ref):
     sections = keep_ref.shape[1]
     head = scal_ref.shape[1]
-    rows, width = x_ref.shape
+    rows, width = keep_ref.shape[0], x_ref.shape[1]
     wide = 4 * head
-    x_float = x_ref[...].astype(F32)
+    start = pl.multiple_of(lax.axis_index("section") * rows, rows)
+    x_float = x_ref[pl.ds(start, rows), :].astype(F32)
     square = jnp.sum(x_float * x_float, axis=1, keepdims=True)
     z = [jnp.sum(z_ref[s].astype(F32), axis=0) for s in range(sections)]
     base = sections // 2 * 3 * head
@@ -759,10 +783,6 @@
     chips = reps // 2
     rows = batches * ROWS
     wide = 4 * head
-    x_own = lax.dynamic_slice_in_dim(x_in, section_pos * rows, rows, 0)
-    c_own = lax.dynamic_slice_in_dim(cot, section_pos * rows, rows, 0)
-    x_split = x_own.reshape(rows, reps, shard).swapaxes(0, 1)
-    c_split = c_own.reshape(rows, reps, shard).swapaxes(0, 1)
     w_pack = jnp.concatenate([w_q[0], w_k[0], w_v[0], w_out[0]], axis=1)
     g_own = lax.dynamic_slice_in_dim(gains, rep_pos * shard, shard, 1)
     running = jnp.zeros_like(offsets[0])
@@ -783,14 +803,14 @@
     keep = jnp.broadcast_to(keep[:, :, None, :], (reps, batches, ROWS, sections))
     keep = keep.reshape(reps * rows, sections)
     keep_own = lax.dynamic_slice_in_dim(keep, slot("rep", rep_pos, reps) * rows, rows, 0)
-    x_shard, c_shard, w_all, g_all, z, mixed = front_call(x_split, c_split, w_pack, g_own, 0)
+    x_shard, c_shard, w_all, g_all, z, mixed = front_call(x_in, cot, w_pack, g_own, rows, 0)
     made, scal = local_call(
         functools.partial(chain_kernel, head ** (-0.5)),
         [
             jax.ShapeDtypeStruct((4, rows, sections * head), BF16),
             jax.ShapeDtypeStruct((rows, head), F32),
         ],
-        x_own,
+        x_in,
         z,
         mixed,
         keep_own,
@@ -803,7 +823,7 @@
     sections = lax.axis_size("section")
     head = arrays[2].shape[2]
     reps = lax.axis_size("rep")
-    if sections == 4 and reps % 2 == 0 and head % (16 * reps) == 0:
+    if sections == 4 and reps == 8 and head % (16 * reps) == 0:
         return low_rank(*arrays)
     return pipelined(*arrays)
 

time: 104 us -> 103 us (level)
  local copies, waits for them, and re-layouts: 6.28 us -> 3.58 us
  other arithmetic: 1.35 us -> 2.44 us
    reshape x2 -> x0, local copies, waits for them, and re-layouts: 1.51 us -> none  [the longest x1 0.78 us: low_rank(): x_split = x_own.reshape(rows, reps, shard).swapaxes(0, 1)]
    dynamic_slice x1 -> x0, local copies, waits for them, and re-layouts: 1.17 us -> none  [low_rank(): c_own = lax.dynamic_slice_in_dim(cot, section_pos * rows, rows, 0)]
    concatenate x1, other arithmetic: 0.86 us -> 1.95 us  [low_rank(): w_pack = jnp.concatenate([w_q[0], w_k[0], w_v[0], w_out[0]], axis=1)]
where the time goes in v5:
time: 103 us
  Pallas kernels  96 us (93%)
  local copies, waits for them, and re-layouts  3.58 us (3%)
  other arithmetic  2.44 us (2%)
    pallas_call x1, Pallas kernels, front_call(): pl.pallas_call(front_kernel, out_shape=[jax.ShapeDtypeStruct((reps, rows,...  50.3 us
    pallas_call x1, Pallas kernels, tail_call(): pl.pallas_call(tail_kernel, out_shape=[jax.ShapeDtypeStruct((4, shard, he...  39.3 us
    pallas_call x1, Pallas kernels, local_call(): pl.pallas_call(kernel, out_shape=shapes, in_specs=vmem_specs(len(arrays))...  6.33 us
    slice x1, local copies, waits for them, and re-layouts, low_rank(): return tuple((grads[i][None] for i in range(4)))  2.17 us

profile of v5, /device:TPU:0, one launch (start us, length us, event | category | flops | bytes accessed | tf_op | source)
XLA Modules:
  0.0 102.7 jit_solution(8732627031857995393)
XLA Ops:
  0.6 0.0 copy-start
  0.6 0.0 copy-start.2
  0.7 0.0 copy-start.3
  0.7 2.0 %pad_maximum_fusion.w_in = bf16[512,512]{1,0:T(8,128)(2,1)} fusion(bf16[512,128]{1,0:T(8,128)(2,1)} %bitcast.9, bf16[512,128]{1,0:T(8,128)(2,1)} %bitcast.10, bf16[512,128]{1,0:T(8,128)(2,1)} %bitcast.11, bf16[512,128]{1,0:T(8,128)(2,1)} %bitcast.12), kind=kLoop, calls=%fused_computation | loop fusion | flops 2097152 | bytes 1048576 | tf_op jit(solution)/shard_map/concatenate | solution.py:786
  2.6 0.0 copy-done
  2.6 0.6 constant_dynamic-slice_fusion.2.g_in
  3.2 50.3 %shard_map.120 = (bf16[8,32,512]{2,1,0:T(8,128)(2,1)}, bf16[8,32,512]{2,1,0:T(8,128)(2,1)}, bf16[4,512,512]{2,1,0:T(8,128)(2,1)}, f32[4,1,512]{2,1,0:T(1,128)}, ...) custom-call(bf16[128,4096]{1,0:T(8,128)(2,1)} %x_ref.1, bf16[128,4096]{1,0:T(8,128)(2,1)} %c_in.1, ...), custom_call_target="tpu_custom_call" | custom-call | tf_op jit(solution)/shard_map/pallas_call | solution.py:476
  53.5 0.0 copy-done.3
  53.6 0.1 constant_dynamic-slice_fusion.1
  53.6 0.1 and_select_fusion
  53.7 0.0 copy-done.2
  53.7 0.3 select_reduce_fusion
  54.0 0.1 fusion.1
  54.1 0.1 copy.13
  54.2 0.0 copy-start.1
  54.3 0.6 constant_dynamic-slice_fusion.keep_ref
  54.9 6.3 %shard_map.121 = (bf16[4,32,512]{2,1,0:T(8,128)(2,1)}, f32[32,128]{1,0:T(8,128)}) custom-call(bf16[128,4096]{1,0:T(8,128)(2,1)} %x_ref.1, bf16[4,2,32,640]{3,2,1,0:T(8,128)(2,1)} %get-tuple-element.14.z_ref, bf16[2,4,4,16,1280]{4,3,2,1,0:T(8,128)(2,1)} %get-tuple-element.15.m_ref, f32[32,4]{1,0:T(8,128)} %constant_dynamic-slice_fusion.keep_ref), custom_call_target="tpu_custom_call" | custom-call | tf_op jit(solution)/shard_map/pallas_call | solution.py:766
  61.2 0.0 copy-done.1
  61.2 39.3 %shard_map.122 = f32[4,512,128]{2,1,0:T(8,128)} custom-call(bf16[8,32,512]{2,1,0:T(8,128)(2,1)} %get-tuple-element.12.x_ref, bf16[8,32,512]{2,1,0:T(8,128)(2,1)} %get-tuple-element.13.c_ref, bf16[4,32,512]{2,1,0:T(8,128)(2,1)} %get-tuple-element.16.made_ref, f32[32,128]{1,0:T(8,128)} %get-tuple-element.17.scal_ref, f32[256,4]{1,0:T(8,128)} %bitcast.8, ...), custom_call_target="tpu_custom_call" | custom-call | tf_op jit(solution)/shard_map/pallas_call | solution.py:741
  100.6 2.2 %fusion.8 = (f32[1,512,128]{2,1,0:T(8,128)}, f32[1,512,128]{2,1,0:T(8,128)}, f32[1,512,128]{2,1,0:T(8,128)}, f32[1,512,128]{2,1,0:T(8,128)}) fusion(f32[4,512,128]{2,1,0:T(8,128)} %shard_map.122), kind=kLoop, calls=%fused_computation.40 | loop fusion | bytes 2097152 | tf_op jit(solution)/shard_map/slice | solution.py:819
  (5 shorter events, 0.1 us)
Async XLA Ops:
  0.6 2.0 %copy-start = (f32[1,4096]{1,0:T(1,128)S(1)}, f32[1,4096]{1,0:T(1,128)}, u32[]{:S(2)}) copy-start(f32[1,4096]{1,0:T(1,128)} %param.15) | copy-start | bytes 49156
  0.6 53.1 %copy-start.2 = (s32[4,8]{1,0:T(4,128)S(1)}, s32[4,8]{1,0:T(4,128)}, u32[]{:S(2)}) copy-start(s32[4,8]{1,0:T(4,128)} %param.17) | copy-start | bytes 388
  0.7 52.9 %copy-start.3 = (s32[4,8]{1,0:T(4,128)S(1)}, s32[4,8]{1,0:T(4,128)}, u32[]{:S(2)}) copy-start(s32[4,8]{1,0:T(4,128)} %param.16) | copy-start | bytes 388
  54.2 7.0 %copy-start.1 = (f32[8,2,16,4]{3,2,1,0:T(8,128)}, f32[8,2,16,4]{3,2,1,0:T(8,128)S(1)}, u32[]{:S(2)}) copy-start(f32[8,2,16,4]{3,2,1,0:T(8,128)S(1)} %broadcast_in_dim.16) | copy-start | bytes 12292
